TPU v7x, 32 devices: a whole 2x2x4 slice. The times are simulated.
32 devices in a mesh: grp: 2 (over y), ka: 4 (over z), vib: 2 (over core), fin: 2 (over x).
Axes of the slice: x: 2, y: 2, z: 4, core: 2. Of those that a mesh axis runs over, the one named last changes fastest.
Arguments:
- moments: bfloat16 [2, 2048, 2048], P(None, 'vib'), may hold values from -0.125 to 0.125
- initial_vectors: bfloat16 [8, 2048, 2048], P('ka', 'vib', 'grp'), parts along dimension 2, may hold values from -6 to 6
- final_vectors: bfloat16 [8, 2048, 1024], P('ka', 'vib', ('grp', 'fin')), parts along dimension 2, may hold values from -0.046875 to 0.046875
- basis_counts: int32 [16], P(('grp', 'ka')), parts along dimension 0, may hold values from 512 to 2048
Outputs:
- strengths: float32 [2048, 512], P(('grp', 'ka', 'vib'), 'fin'), parts along dimension 0
There are 2 independent parts, one for each index of `grp`. A program takes and returns all parts, laid end to end along the dimension named above; an argument that names none is the same for every part. Nothing has to cross between parts.
All inputs are finite; a program needn't handle non-finite values.
Results may differ from a plain program's by a relative error of at most 0.0003.
Values may be sent and summed in bfloat16 or wider, within the bound.
A program may use at most 64 MiB of HBM per device.

v0:
```python
import functools

import jax
import jax.numpy as jnp
from jax import lax
from jax.experimental import pallas as pl
from jax.experimental.pallas import tpu as pltpu
from jax.sharding import PartitionSpec as P

JQ = 30
MESH = pl.DeviceIdType.MESH
F32 = jnp.float32
BF16 = jnp.bfloat16


def coefficient_rows(index, width):
    value = jnp.full((1, width), index, jnp.int32).astype(F32)
    jsquare = float(JQ * (JQ + 1))
    norm_j = jnp.sqrt(jnp.full((1, width), jsquare, F32))
    same = value / norm_j
    upper = 0.5 * jnp.sqrt(jsquare - value * (value + 1.0)) / norm_j
    lower = -0.5 * jnp.sqrt(jsquare - value * (value - 1.0)) / norm_j
    return same, upper, lower


def kernel(
    n_ka, n_half, chunks, counts_ref, moments_hbm, initial_hbm, final_hbm, out_ref,
    mom, ini, raw, own, edge, comb, split, amp, part, zsend, zrecv,
    mom_sem, ini_sem, raw_sem, own_send, own_recv, z_send, z_recv,
    fwd_send, fwd_recv, part_send, part_recv, out_send, out_recv,
):
    kblocks, rows, width = raw.shape
    states = ini.shape[2]
    share = out_ref.shape[0]
    whole = mom.shape[2]
    half = width // n_half
    a = lax.axis_index("ka")
    b = lax.axis_index("vib")
    other = 1 - b
    first = a * kblocks - kblocks * n_ka // 2

    get_final = pltpu.make_async_copy(final_hbm, raw, raw_sem)
    get_final.start()
    cores = (b, other)

    def cols_of(core):
        return pl.ds(pl.multiple_of(core * rows, rows), rows)

    def get_moments(i, c):
        span = cols_of(cores[i])
        return pltpu.make_async_copy(
            moments_hbm.at[c, :, span], mom.at[c, :, span], mom_sem.at[i, c]
        )

    for i in range(2):
        for c in range(2):
            get_moments(i, c).start()
    get_initial = pltpu.make_async_copy(initial_hbm, ini, ini_sem)
    get_initial.start()

    barrier = pltpu.get_barrier_semaphore()
    pl.semaphore_signal(barrier, inc=1, device_id={"vib": other}, device_id_type=MESH)
    for d in range(1, n_ka):
        pl.semaphore_signal(
            barrier, inc=1, device_id={"ka": lax.rem(a + d, n_ka)}, device_id_type=MESH
        )

    get_final.wait()
    own_rows = cols_of(b)
    row_index = lax.broadcasted_iota(jnp.int32, (rows, half), 0) + b * rows
    for h in range(n_half):
        for k in range(kblocks):
            live = row_index < counts_ref[k]
            piece = raw[k, :, h * half : (h + 1) * half].astype(F32)
            own[h, own_rows, k * half : (k + 1) * half] = jnp.where(live, piece, 0.0).astype(BF16)

    has_up = a < n_ka - 1
    has_down = a > 0
    pl.semaphore_wait(barrier, n_ka)

    step = rows // chunks

    def at(core, j):
        return pl.ds(pl.multiple_of(core * rows + j * step, step), step)

    def side_lanes(side):
        return pl.ds(side * half, half)

    def z_copy(side, h, j):
        to = a + 1 if side == 0 else a - 1
        return pltpu.make_async_remote_copy(
            src_ref=own.at[h, at(b, j), side_lanes(1 - side)],
            dst_ref=edge.at[h, at(b, j), side_lanes(side)],
            send_sem=z_send.at[side, h, j],
            recv_sem=z_recv.at[side, h, j],
            device_id={"ka": to},
            device_id_type=MESH,
        )

    def forward(side, h, j):
        return pltpu.make_async_remote_copy(
            src_ref=edge.at[h, at(b, j), side_lanes(side)],
            dst_ref=edge.at[h, at(b, j), side_lanes(side)],
            send_sem=fwd_send.at[side, h, j],
            recv_sem=fwd_recv.at[side, h, j],
            device_id={"vib": other},
            device_id_type=MESH,
        )

    def own_copy(h):
        return pltpu.make_async_remote_copy(
            src_ref=own.at[h, own_rows],
            dst_ref=own.at[h, own_rows],
            send_sem=own_send.at[h],
            recv_sem=own_recv.at[h],
            device_id={"vib": other},
            device_id_type=MESH,
        )

    sends = (has_up, has_down)
    takes = (has_down, has_up)
    for h in range(n_half):
        for j in range(chunks):
            for side in range(2):
                @pl.when(sends[side])
                def _():
                    z_copy(side, h, j).start()
        own_copy(h).start()
    for side in range(2):
        @pl.when(jnp.logical_not(takes[side]))
        def _():
            for h in range(n_half):
                edge[h, :, side * half : (side + 1) * half] = jnp.zeros((whole, half), BF16)

    same0, upper0, _ = coefficient_rows(first, half)
    same1, _, lower1 = coefficient_rows(first + 1, half)
    _, upper_below, _ = coefficient_rows(first - 1, half)
    _, _, lower_above = coefficient_rows(first + 2, half)
    same_row = jnp.concatenate([same0, same1], axis=1)
    cross_row = jnp.concatenate([lower1, upper0], axis=1)
    edge_row = jnp.concatenate([upper_below, lower_above], axis=1)

    def relay(h, j):
        for side in range(2):
            @pl.when(takes[side])
            def _():
                z_copy(side, h, j).wait_recv()
                forward(side, h, j).start()

    tile = rows // 2
    for i in range(2):
        for c in range(2):
            get_moments(i, c).wait()
        for h in range(n_half):
            if i == 1:
                own_copy(h).wait_recv()
            piece = own[h, cols_of(cores[i]), :]
            for t in range(2):
                span = pl.ds(t * tile, tile)
                along_z = jnp.dot(
                    mom[0, span, cols_of(cores[i])], piece, preferred_element_type=F32
                )
                along_x = jnp.dot(
                    mom[1, span, cols_of(cores[i])], piece, preferred_element_type=F32
                )
                crossed = jnp.concatenate([along_x[:, half:], along_x[:, :half]], axis=1)
                value = same_row * along_z + cross_row * crossed
                comb[h, span, :] = value if i == 0 else comb[h, span, :] + value

    def take(h, core, j):
        piece = edge[h, at(core, j), :]
        for t in range(2):
            span = pl.ds(t * tile, tile)
            comb[h, span, :] = comb[h, span, :] + edge_row * jnp.dot(
                mom[1, span, at(core, j)], piece, preferred_element_type=F32
            )

    block = min(256, rows)
    lane_index = lax.broadcasted_iota(jnp.int32, (half, block), 1) + b * rows

    def split_half(h):
        for t in range(rows // block):
            both = comb[h, pl.ds(t * block, block), :].T
            for k in range(kblocks):
                turned = both[k * half : (k + 1) * half]
                turned = jnp.where(lane_index + t * block < counts_ref[k], turned, 0.0)
                high = turned.astype(BF16)
                low = (turned - high.astype(F32)).astype(BF16)
                split[h, k, pl.ds(0, half), pl.ds(t * block, block)] = high
                split[h, k, pl.ds(half, half), pl.ds(t * block, block)] = low

    lanes = min(256, states)
    n_blocks = states // lanes
    targets = lanes // (2 * share)
    own_block = a // targets if targets > 1 else a

    toward = 2 * ((2 * a) // n_ka) - 1

    def block_of(s):
        return lax.rem(own_block + toward * (1 + s) + n_blocks, n_blocks)

    def part_copy(h, s):
        size = targets * share
        span = pl.ds(pl.multiple_of(block_of(s) * size, size), size)
        return pltpu.make_async_remote_copy(
            src_ref=amp.at[h, other, span],
            dst_ref=part.at[h, span],
            send_sem=part_send.at[h, s],
            recv_sem=part_recv.at[h, s],
            device_id={"vib": other},
            device_id_type=MESH,
        )

    def out_copy(h, target, slot):
        return pltpu.make_async_remote_copy(
            src_ref=zsend.at[h, slot],
            dst_ref=zrecv.at[h, a],
            send_sem=out_send.at[h, slot],
            recv_sem=out_recv.at[h, a],
            device_id={"ka": target},
            device_id_type=MESH,
        )

    def finish(h, s):
        part_copy(h, s).wait_recv()
        for j in range(targets):
            target = block_of(s) * targets + j
            span = pl.ds(pl.multiple_of(target * share, share), share)
            slot = s * targets + j
            value = amp[h, b, span, :] + part[h, span, :]
            zsend[h, slot] = value

            @pl.when(target == a)
            def _():
                out_ref[:, h * half : (h + 1) * half] = value

            @pl.when(target != a)
            def _():
                out_copy(h, target, slot).start()

    def amplitude_block(h, s):
        cols = pl.ds(pl.multiple_of(block_of(s) * lanes, lanes), lanes)
        both = jnp.dot(split[h, 0], ini[0, :, cols], preferred_element_type=F32)
        for k in range(1, kblocks):
            both = both + jnp.dot(split[h, k], ini[k, :, cols], preferred_element_type=F32)
        value = (both[:half] + both[half:]).T
        for j in range(targets):
            for core in range(2):
                low = (j * 2 + core) * share
                target = block_of(s) * targets + j
                amp[h, core, pl.ds(pl.multiple_of(target * share, share), share), :] = value[
                    low : low + share
                ]
        part_copy(h, s).start()

    for h in range(n_half):
        for j in range(chunks):
            if h == 0 or j > 0:
                relay(h, j)
            take(h, b, j)
        for j in range(chunks):
            for side in range(2):
                @pl.when(takes[side])
                def _():
                    forward(side, h, j).wait_recv()
            take(h, other, j)
        split_half(h)
        if h == 0:
            get_initial.wait()
        for s in range(n_blocks):
            amplitude_block(h, s)
            if s > 0:
                finish(h, s - 1)
            if s == n_blocks // 2 and h + 1 < n_half:
                relay(h + 1, 0)
    for h in range(n_half):
        finish(h, n_blocks - 1)

    for h in range(n_half):
        for d in range(1, n_ka):
            sender = lax.rem(a + d, n_ka)
            pltpu.make_async_remote_copy(
                src_ref=zsend.at[h, 0],
                dst_ref=zrecv.at[h, sender],
                send_sem=out_send.at[h, 0],
                recv_sem=out_recv.at[h, sender],
                device_id={"ka": sender},
                device_id_type=MESH,
            ).wait_recv()
            lanes_h = pl.ds(h * half, half)
            out_ref[:, lanes_h] = out_ref[:, lanes_h] + zrecv[h, sender]

    for h in range(n_half):
        own_copy(h).wait_send()
        for j in range(chunks):
            for side in range(2):
                @pl.when(sends[side])
                def _():
                    z_copy(side, h, j).wait_send()

                @pl.when(takes[side])
                def _():
                    forward(side, h, j).wait_send()
        for s in range(n_blocks):
            part_copy(h, s).wait_send()
            for j in range(targets):
                target = block_of(s) * targets + j

                @pl.when(target != a)
                def _():
                    out_copy(h, target, s * targets + j).wait_send()


def on_device(n_ka, moments, initial_vectors, final_vectors, basis_counts):
    kblocks, rows, states = initial_vectors.shape
    width = final_vectors.shape[2]
    whole = moments.shape[2]
    share = states // (2 * n_ka)
    n_half = max(1, width // 128)
    half = width // n_half
    chunks = 2
    dma = pltpu.SemaphoreType.DMA
    n_blocks = states // min(256, states)
    amplitude = pl.pallas_call(
        functools.partial(kernel, n_ka, n_half, chunks),
        out_shape=jax.ShapeDtypeStruct((share, width), F32),
        in_specs=[pl.BlockSpec(memory_space=pltpu.SMEM)]
        + [pl.BlockSpec(memory_space=pl.ANY)] * 3,
        out_specs=pl.BlockSpec(memory_space=pltpu.VMEM),
        scratch_shapes=[
            pltpu.VMEM(moments.shape, BF16),
            pltpu.VMEM(initial_vectors.shape, BF16),
            pltpu.VMEM(final_vectors.shape, BF16),
            pltpu.VMEM((n_half, whole, kblocks * half), BF16),
            pltpu.VMEM((n_half, whole, 2 * half), BF16),
            pltpu.VMEM((n_half, rows, kblocks * half), F32),
            pltpu.VMEM((n_half, kblocks, 2 * half, rows), BF16),
            pltpu.VMEM((n_half, 2, n_ka * share, half), F32),
            pltpu.VMEM((n_half, n_ka * share, half), F32),
            pltpu.VMEM((n_half, n_ka, share, half), F32),
            pltpu.VMEM((n_half, n_ka, share, half), F32),
            dma((2, 2)),
            dma(()),
            dma(()),
            dma((n_half,)),
            dma((n_half,)),
            dma((2, n_half, chunks)),
            dma((2, n_half, chunks)),
            dma((2, n_half, chunks)),
            dma((2, n_half, chunks)),
            dma((n_half, n_blocks)),
            dma((n_half, n_blocks)),
            dma((n_half, n_ka)),
            dma((n_half, n_ka)),
        ],
        compiler_params=pltpu.CompilerParams(
            collective_id=0, has_side_effects=True, vmem_limit_bytes=60 * 2**20
        ),
    )(basis_counts, moments, initial_vectors, final_vectors)
    return amplitude * amplitude


def solution(mesh):
    in_specs = (
        P(None, "vib", None),
        P("ka", "vib", "grp"),
        P("ka", "vib", ("grp", "fin")),
        P(("grp", "ka")),
    )
    out_specs = P(("grp", "ka", "vib"), "fin")
    return jax.shard_map(
        functools.partial(on_device, mesh.shape["ka"]),
        mesh=mesh, in_specs=in_specs, out_specs=out_specs, check_vma=False,
    )
```

profile of v0, /device:TPU:0, one launch (start us, length us, event | category | flops | bytes accessed | tf_op | source)
XLA Modules:
  0.0 32.3 jit_solution(18351532081021488222)
XLA Ops:
  0.0 30.7 %shard_map.46 = f32[128,256]{1,0:T(8,128)} custom-call(s32[2]{0:T(128)} %counts_ref.1, bf16[2,1024,2048]{2,1,0:T(8,128)(2,1)} %moments_hbm.1, bf16[2,1024,1024]{2,1,0:T(8,128)(2,1)} %initial_hbm.1, bf16[2,1024,256]{2,1,0:T(8,128)(2,1)} %final_hbm.1), custom_call_target="tpu_custom_call" | custom-call | tf_op jit(solution)/shard_map/pallas_call | solution.py:324
  30.7 1.7 %mul.3 = f32[128,256]{1,0:T(8,128)} multiply(f32[128,256]{1,0:T(8,128)} %shard_map.46, f32[128,256]{1,0:T(8,128)} %shard_map.46) | non-fusion elementwise | flops 32768 | bytes 393216 | tf_op jit(solution)/shard_map/mul | solution.py:360
where the time goes:
time: 32.5 us; the launch traced here: 32.3 us
  Pallas kernels  30.7 us (94%)
  other arithmetic  1.65 us (5%)
    pallas_call x1, Pallas kernels, on_device(): pl.pallas_call(functools.partial(kernel, n_ka, n_half, chunks), out_shape...  30.7 us
    mul x1, other arithmetic, on_device(): return amplitude * amplitude  1.65 us

commit v1 on v0

--- a/solution.py
+++ b/solution.py
@@ -11,6 +11,8 @@
 MESH = pl.DeviceIdType.MESH
 F32 = jnp.float32
 BF16 = jnp.bfloat16
+LEVELS = 32767.0
+TINY = 1e-30
 
 
 def coefficient_rows(index, width):
@@ -25,9 +27,10 @@
 
 def kernel(
     n_ka, n_half, chunks, counts_ref, moments_hbm, initial_hbm, final_hbm, out_ref,
-    mom, ini, raw, own, edge, comb, split, amp, part, zsend, zrecv,
+    mom, ini, raw, own, edge, comb, split, amp, part, zsend, zrecv, ssend, srecv,
     mom_sem, ini_sem, raw_sem, own_send, own_recv, z_send, z_recv,
-    fwd_send, fwd_recv, part_send, part_recv, out_send, out_recv,
+    fwd_send, fwd_recv, part_send, part_recv, out_send, out_recv, scale_send, scale_recv,
+    token_up, token_down,
 ):
     kblocks, rows, width = raw.shape
     states = ini.shape[2]
@@ -39,8 +42,17 @@
     other = 1 - b
     first = a * kblocks - kblocks * n_ka // 2
 
-    get_final = pltpu.make_async_copy(final_hbm, raw, raw_sem)
-    get_final.start()
+    step = rows // chunks
+
+    def get_final(h, j):
+        span, lanes_h = pl.ds(j * step, step), pl.ds(h * half, half)
+        return pltpu.make_async_copy(
+            final_hbm.at[:, span, lanes_h], raw.at[:, span, lanes_h], raw_sem.at[h, j]
+        )
+
+    for h in range(n_half):
+        for j in range(chunks):
+            get_final(h, j).start()
     cores = (b, other)
 
     def cols_of(core):
@@ -58,27 +70,30 @@
     get_initial = pltpu.make_async_copy(initial_hbm, ini, ini_sem)
     get_initial.start()
 
+    has_up = a < n_ka - 1
+    has_down = a > 0
+    sends = (has_up, has_down)
+    takes = (has_down, has_up)
+    toward_side = (a + 1, a - 1)
+
     barrier = pltpu.get_barrier_semaphore()
     pl.semaphore_signal(barrier, inc=1, device_id={"vib": other}, device_id_type=MESH)
-    for d in range(1, n_ka):
-        pl.semaphore_signal(
-            barrier, inc=1, device_id={"ka": lax.rem(a + d, n_ka)}, device_id_type=MESH
-        )
-
-    get_final.wait()
+    for side in range(2):
+        @pl.when(sends[side])
+        def _():
+            pl.semaphore_signal(
+                barrier, inc=1, device_id={"ka": toward_side[side]}, device_id_type=MESH
+            )
+
     own_rows = cols_of(b)
-    row_index = lax.broadcasted_iota(jnp.int32, (rows, half), 0) + b * rows
-    for h in range(n_half):
+    row_index = lax.broadcasted_iota(jnp.int32, (step, half), 0) + b * rows
+
+    def mask_final(h, j):
+        get_final(h, j).wait()
         for k in range(kblocks):
-            live = row_index < counts_ref[k]
-            piece = raw[k, :, h * half : (h + 1) * half].astype(F32)
-            own[h, own_rows, k * half : (k + 1) * half] = jnp.where(live, piece, 0.0).astype(BF16)
-
-    has_up = a < n_ka - 1
-    has_down = a > 0
-    pl.semaphore_wait(barrier, n_ka)
-
-    step = rows // chunks
+            live = row_index + j * step < counts_ref[k]
+            piece = raw[k, j * step : (j + 1) * step, h * half : (h + 1) * half].astype(F32)
+            own[h, at(b, j), k * half : (k + 1) * half] = jnp.where(live, piece, 0.0).astype(BF16)
 
     def at(core, j):
         return pl.ds(pl.multiple_of(core * rows + j * step, step), step)
@@ -87,13 +102,12 @@
         return pl.ds(side * half, half)
 
     def z_copy(side, h, j):
-        to = a + 1 if side == 0 else a - 1
         return pltpu.make_async_remote_copy(
             src_ref=own.at[h, at(b, j), side_lanes(1 - side)],
             dst_ref=edge.at[h, at(b, j), side_lanes(side)],
             send_sem=z_send.at[side, h, j],
             recv_sem=z_recv.at[side, h, j],
-            device_id={"ka": to},
+            device_id={"ka": toward_side[side]},
             device_id_type=MESH,
         )
 
@@ -117,10 +131,12 @@
             device_id_type=MESH,
         )
 
-    sends = (has_up, has_down)
-    takes = (has_down, has_up)
+    mask_final(0, 0)
+    pl.semaphore_wait(barrier, 1 + has_up.astype(jnp.int32) + has_down.astype(jnp.int32))
     for h in range(n_half):
         for j in range(chunks):
+            if h + j > 0:
+                mask_final(h, j)
             for side in range(2):
                 @pl.when(sends[side])
                 def _():
@@ -211,15 +227,44 @@
             device_id_type=MESH,
         )
 
-    def out_copy(h, target, slot):
-        return pltpu.make_async_remote_copy(
+    def out_copies(h, sender, target, slot):
+        values = pltpu.make_async_remote_copy(
             src_ref=zsend.at[h, slot],
-            dst_ref=zrecv.at[h, a],
+            dst_ref=zrecv.at[h, sender],
             send_sem=out_send.at[h, slot],
-            recv_sem=out_recv.at[h, a],
+            recv_sem=out_recv.at[h, sender],
             device_id={"ka": target},
             device_id_type=MESH,
         )
+        scales = pltpu.make_async_remote_copy(
+            src_ref=ssend.at[h, slot],
+            dst_ref=srecv.at[h, sender],
+            send_sem=scale_send.at[h, slot],
+            recv_sem=scale_recv.at[h, sender],
+            device_id={"ka": target},
+            device_id_type=MESH,
+        )
+        return values, scales
+
+    def token(side, r):
+        to = toward_side[side]
+        sem = (token_up, token_down)[side]
+        about = a - 1 - r if side == 0 else a + 1 + r
+        known = about >= 0 if side == 0 else about <= n_ka - 1
+
+        @pl.when(jnp.logical_and(known, sends[side]))
+        def _():
+            pl.semaphore_signal(sem.at[r - 1], inc=1, device_id={"ka": to}, device_id_type=MESH)
+
+    def await_token(side, r):
+        sem = (token_up, token_down)[side]
+        told = a - 2 - r >= 0 if side == 0 else a + 2 + r <= n_ka - 1
+
+        @pl.when(told)
+        def _():
+            pl.semaphore_wait(sem.at[r - 1], 1)
+
+    rounds = max(0, n_ka - 3)
 
     def finish(h, s):
         part_copy(h, s).wait_recv()
@@ -228,7 +273,6 @@
             span = pl.ds(pl.multiple_of(target * share, share), share)
             slot = s * targets + j
             value = amp[h, b, span, :] + part[h, span, :]
-            zsend[h, slot] = value
 
             @pl.when(target == a)
             def _():
@@ -236,7 +280,11 @@
 
             @pl.when(target != a)
             def _():
-                out_copy(h, target, slot).start()
+                peak = jnp.maximum(jnp.max(jnp.abs(value), axis=0, keepdims=True), TINY)
+                zsend[h, slot] = jnp.round(value * (LEVELS / peak)).astype(jnp.int16)
+                ssend[h, slot] = jnp.broadcast_to(peak / LEVELS, (8, half))
+                for copy in out_copies(h, a, target, slot):
+                    copy.start()
 
     def amplitude_block(h, s):
         cols = pl.ds(pl.multiple_of(block_of(s) * lanes, lanes), lanes)
@@ -257,6 +305,9 @@
         for j in range(chunks):
             if h == 0 or j > 0:
                 relay(h, j)
+            if h + j == 0 and rounds > 0:
+                for side in range(2):
+                    token(side, 1)
             take(h, b, j)
         for j in range(chunks):
             for side in range(2):
@@ -267,6 +318,12 @@
         split_half(h)
         if h == 0:
             get_initial.wait()
+            for r in range(1, rounds + 1):
+                for side in range(2):
+                    if r > 1:
+                        token(side, r)
+                for side in range(2):
+                    await_token(side, r)
         for s in range(n_blocks):
             amplitude_block(h, s)
             if s > 0:
@@ -279,16 +336,12 @@
     for h in range(n_half):
         for d in range(1, n_ka):
             sender = lax.rem(a + d, n_ka)
-            pltpu.make_async_remote_copy(
-                src_ref=zsend.at[h, 0],
-                dst_ref=zrecv.at[h, sender],
-                send_sem=out_send.at[h, 0],
-                recv_sem=out_recv.at[h, sender],
-                device_id={"ka": sender},
-                device_id_type=MESH,
-            ).wait_recv()
+            for copy in out_copies(h, sender, sender, 0):
+                copy.wait_recv()
             lanes_h = pl.ds(h * half, half)
-            out_ref[:, lanes_h] = out_ref[:, lanes_h] + zrecv[h, sender]
+            out_ref[:, lanes_h] = out_ref[:, lanes_h] + (
+                zrecv[h, sender].astype(F32) * srecv[h, sender, 0:1, :]
+            )
 
     for h in range(n_half):
         own_copy(h).wait_send()
@@ -308,7 +361,8 @@
 
                 @pl.when(target != a)
                 def _():
-                    out_copy(h, target, s * targets + j).wait_send()
+                    for copy in out_copies(h, a, target, s * targets + j):
+                        copy.wait_send()
 
 
 def on_device(n_ka, moments, initial_vectors, final_vectors, basis_counts):
@@ -337,11 +391,13 @@
             pltpu.VMEM((n_half, kblocks, 2 * half, rows), BF16),
             pltpu.VMEM((n_half, 2, n_ka * share, half), F32),
             pltpu.VMEM((n_half, n_ka * share, half), F32),
-            pltpu.VMEM((n_half, n_ka, share, half), F32),
-            pltpu.VMEM((n_half, n_ka, share, half), F32),
+            pltpu.VMEM((n_half, n_ka, share, half), jnp.int16),
+            pltpu.VMEM((n_half, n_ka, share, half), jnp.int16),
+            pltpu.VMEM((n_half, n_ka, 8, half), F32),
+            pltpu.VMEM((n_half, n_ka, 8, half), F32),
             dma((2, 2)),
             dma(()),
-            dma(()),
+            dma((n_half, chunks)),
             dma((n_half,)),
             dma((n_half,)),
             dma((2, n_half, chunks)),
@@ -352,6 +408,10 @@
             dma((n_half, n_blocks)),
             dma((n_half, n_ka)),
             dma((n_half, n_ka)),
+            dma((n_half, n_ka)),
+            dma((n_half, n_ka)),
+            pltpu.SemaphoreType.REGULAR((max(1, n_ka - 3),)),
+            pltpu.SemaphoreType.REGULAR((max(1, n_ka - 3),)),
         ],
         compiler_params=pltpu.CompilerParams(
             collective_id=0, has_side_effects=True, vmem_limit_bytes=60 * 2**20

time: 32.5 us -> 31 us (0.954)
  Pallas kernels: 30.7 us -> 29.1 us
    pallas_call x1, Pallas kernels: 30.7 us -> 29.1 us  [on_device(): pl.pallas_call(functools.partial(kernel, n_ka, n_half, chunks), out_shape...]
where the time goes in v1:
time: 31 us; the launch traced here: 30.8 us
  Pallas kernels  29.1 us (94%)
  other arithmetic  1.65 us (5%)
    pallas_call x1, Pallas kernels, on_device(): pl.pallas_call(functools.partial(kernel, n_ka, n_half, chunks), out_shape...  29.1 us
    mul x1, other arithmetic, on_device(): return amplitude * amplitude  1.65 us

profile of v1, /device:TPU:0, one launch (start us, length us, event | category | flops | bytes accessed | tf_op | source)
XLA Modules:
  0.0 30.8 jit_solution(15129486670107078698)
XLA Ops:
  0.0 29.1 %shard_map.46 = f32[128,256]{1,0:T(8,128)} custom-call(s32[2]{0:T(128)} %counts_ref.1, bf16[2,1024,2048]{2,1,0:T(8,128)(2,1)} %moments_hbm.1, bf16[2,1024,1024]{2,1,0:T(8,128)(2,1)} %initial_hbm.1, bf16[2,1024,256]{2,1,0:T(8,128)(2,1)} %final_hbm.1), custom_call_target="tpu_custom_call" | custom-call | tf_op jit(solution)/shard_map/pallas_call | solution.py:378
  29.2 1.7 %mul.3 = f32[128,256]{1,0:T(8,128)} multiply(f32[128,256]{1,0:T(8,128)} %shard_map.46, f32[128,256]{1,0:T(8,128)} %shard_map.46) | non-fusion elementwise | flops 32768 | bytes 393216 | tf_op jit(solution)/shard_map/mul | solution.py:420

commit v2 on v1

--- a/solution.py
+++ b/solution.py
@@ -26,14 +26,14 @@
 
 
 def kernel(
-    n_ka, n_half, chunks, counts_ref, moments_hbm, initial_hbm, final_hbm, out_ref,
-    mom, ini, raw, own, edge, comb, split, amp, part, zsend, zrecv, ssend, srecv,
-    mom_sem, ini_sem, raw_sem, own_send, own_recv, z_send, z_recv,
+    n_ka, n_half, chunks, parts, counts_ref, moments_hbm, initial_hbm, final_hbm, out_ref,
+    mom, ini, turned, own, edge, comb, split, amp, part, zsend, zrecv, ssend, srecv, csend, crecv,
+    mom_sem, ini_sem, own_sem, own_send, own_recv, z_send, z_recv, count_send, count_recv,
     fwd_send, fwd_recv, part_send, part_recv, out_send, out_recv, scale_send, scale_recv,
     token_up, token_down,
 ):
-    kblocks, rows, width = raw.shape
-    states = ini.shape[2]
+    kblocks, rows, states = ini.shape
+    width = final_hbm.shape[2]
     share = out_ref.shape[0]
     whole = mom.shape[2]
     half = width // n_half
@@ -43,16 +43,7 @@
     first = a * kblocks - kblocks * n_ka // 2
 
     step = rows // chunks
-
-    def get_final(h, j):
-        span, lanes_h = pl.ds(j * step, step), pl.ds(h * half, half)
-        return pltpu.make_async_copy(
-            final_hbm.at[:, span, lanes_h], raw.at[:, span, lanes_h], raw_sem.at[h, j]
-        )
-
-    for h in range(n_half):
-        for j in range(chunks):
-            get_final(h, j).start()
+    last = kblocks - 1
     cores = (b, other)
 
     def cols_of(core):
@@ -64,6 +55,17 @@
             moments_hbm.at[c, :, span], mom.at[c, :, span], mom_sem.at[i, c]
         )
 
+    def half_lanes(k):
+        return pl.ds(k * half, half)
+
+    def get_own(h, k):
+        return pltpu.make_async_copy(
+            final_hbm.at[k, :, half_lanes(h)], own.at[h, cols_of(b), half_lanes(k)], own_sem.at[h, k]
+        )
+
+    for h in range(n_half):
+        for k in range(kblocks):
+            get_own(h, k).start()
     for i in range(2):
         for c in range(2):
             get_moments(i, c).start()
@@ -85,68 +87,72 @@
                 barrier, inc=1, device_id={"ka": toward_side[side]}, device_id_type=MESH
             )
 
-    own_rows = cols_of(b)
-    row_index = lax.broadcasted_iota(jnp.int32, (step, half), 0) + b * rows
-
-    def mask_final(h, j):
-        get_final(h, j).wait()
-        for k in range(kblocks):
-            live = row_index + j * step < counts_ref[k]
-            piece = raw[k, j * step : (j + 1) * step, h * half : (h + 1) * half].astype(F32)
-            own[h, at(b, j), k * half : (k + 1) * half] = jnp.where(live, piece, 0.0).astype(BF16)
-
     def at(core, j):
         return pl.ds(pl.multiple_of(core * rows + j * step, step), step)
 
-    def side_lanes(side):
-        return pl.ds(side * half, half)
-
     def z_copy(side, h, j):
         return pltpu.make_async_remote_copy(
-            src_ref=own.at[h, at(b, j), side_lanes(1 - side)],
-            dst_ref=edge.at[h, at(b, j), side_lanes(side)],
+            src_ref=final_hbm.at[last * (1 - side), pl.ds(j * step, step), half_lanes(h)],
+            dst_ref=edge.at[h, at(b, j), half_lanes(side)],
             send_sem=z_send.at[side, h, j],
             recv_sem=z_recv.at[side, h, j],
             device_id={"ka": toward_side[side]},
             device_id_type=MESH,
         )
 
+    def count_copy(side):
+        return pltpu.make_async_remote_copy(
+            src_ref=csend.at[side],
+            dst_ref=crecv.at[side],
+            send_sem=count_send.at[side],
+            recv_sem=count_recv.at[side],
+            device_id={"ka": toward_side[side]},
+            device_id_type=MESH,
+        )
+
     def forward(side, h, j):
         return pltpu.make_async_remote_copy(
-            src_ref=edge.at[h, at(b, j), side_lanes(side)],
-            dst_ref=edge.at[h, at(b, j), side_lanes(side)],
+            src_ref=edge.at[h, at(b, j), half_lanes(side)],
+            dst_ref=edge.at[h, at(b, j), half_lanes(side)],
             send_sem=fwd_send.at[side, h, j],
             recv_sem=fwd_recv.at[side, h, j],
             device_id={"vib": other},
             device_id_type=MESH,
         )
 
-    def own_copy(h):
+    def own_copy(h, k):
         return pltpu.make_async_remote_copy(
-            src_ref=own.at[h, own_rows],
-            dst_ref=own.at[h, own_rows],
-            send_sem=own_send.at[h],
-            recv_sem=own_recv.at[h],
+            src_ref=final_hbm.at[k, :, half_lanes(h)],
+            dst_ref=own.at[h, cols_of(b), half_lanes(k)],
+            send_sem=own_send.at[h, k],
+            recv_sem=own_recv.at[h, k],
             device_id={"vib": other},
             device_id_type=MESH,
         )
 
-    mask_final(0, 0)
+    for side in range(2):
+        csend[side] = jnp.full(csend.shape[1:], counts_ref[last * (1 - side)], jnp.int32)
+
+        @pl.when(jnp.logical_not(takes[side]))
+        def _():
+            crecv[side] = jnp.zeros(crecv.shape[1:], jnp.int32)
+            for h in range(n_half):
+                edge[h, :, side * half : (side + 1) * half] = jnp.zeros((whole, half), BF16)
+
     pl.semaphore_wait(barrier, 1 + has_up.astype(jnp.int32) + has_down.astype(jnp.int32))
+    for side in range(2):
+        @pl.when(sends[side])
+        def _():
+            count_copy(side).start()
     for h in range(n_half):
         for j in range(chunks):
-            if h + j > 0:
-                mask_final(h, j)
             for side in range(2):
                 @pl.when(sends[side])
                 def _():
                     z_copy(side, h, j).start()
-        own_copy(h).start()
-    for side in range(2):
-        @pl.when(jnp.logical_not(takes[side]))
-        def _():
-            for h in range(n_half):
-                edge[h, :, side * half : (side + 1) * half] = jnp.zeros((whole, half), BF16)
+    for h in range(n_half):
+        for k in range(kblocks):
+            own_copy(h, k).start()
 
     same0, upper0, _ = coefficient_rows(first, half)
     same1, _, lower1 = coefficient_rows(first + 1, half)
@@ -165,12 +171,20 @@
 
     tile = rows // 2
     for i in range(2):
-        for c in range(2):
-            get_moments(i, c).wait()
+        row_index = lax.broadcasted_iota(jnp.int32, (rows, half), 0) + cores[i] * rows
         for h in range(n_half):
-            if i == 1:
-                own_copy(h).wait_recv()
-            piece = own[h, cols_of(cores[i]), :]
+            masked = []
+            for k in range(kblocks):
+                if i == 0:
+                    get_own(h, k).wait()
+                else:
+                    own_copy(h, k).wait_recv()
+                piece = own[h, cols_of(cores[i]), half_lanes(k)].astype(F32)
+                masked.append(jnp.where(row_index < counts_ref[k], piece, 0.0).astype(BF16))
+            piece = jnp.concatenate(masked, axis=1)
+            if h == 0:
+                for c in range(2):
+                    get_moments(i, c).wait()
             for t in range(2):
                 span = pl.ds(t * tile, tile)
                 along_z = jnp.dot(
@@ -183,41 +197,52 @@
                 value = same_row * along_z + cross_row * crossed
                 comb[h, span, :] = value if i == 0 else comb[h, span, :] + value
 
+    get_initial.wait()
+    block = min(256, rows)
+    for k in range(kblocks):
+        for v in range(rows // block):
+            low = k * rows + v * block
+            turned[:, low : low + block] = ini[k, v * block : (v + 1) * block, :].T
+
+    for side in range(2):
+        @pl.when(takes[side])
+        def _():
+            count_copy(side).wait_recv()
+    edge_counts = jnp.concatenate([crecv[0, 0:1, :], crecv[1, 0:1, :]], axis=1)
+    edge_index = lax.broadcasted_iota(jnp.int32, (step, 2 * half), 0)
+
     def take(h, core, j):
-        piece = edge[h, at(core, j), :]
+        live = edge_index + (core * rows + j * step) < edge_counts
+        piece = jnp.where(live, edge[h, at(core, j), :].astype(F32), 0.0).astype(BF16)
         for t in range(2):
             span = pl.ds(t * tile, tile)
             comb[h, span, :] = comb[h, span, :] + edge_row * jnp.dot(
                 mom[1, span, at(core, j)], piece, preferred_element_type=F32
             )
 
-    block = min(256, rows)
-    lane_index = lax.broadcasted_iota(jnp.int32, (half, block), 1) + b * rows
+    row_index = lax.broadcasted_iota(jnp.int32, (block, half), 0) + b * rows
 
     def split_half(h):
-        for t in range(rows // block):
-            both = comb[h, pl.ds(t * block, block), :].T
+        for v in range(rows // block):
             for k in range(kblocks):
-                turned = both[k * half : (k + 1) * half]
-                turned = jnp.where(lane_index + t * block < counts_ref[k], turned, 0.0)
-                high = turned.astype(BF16)
-                low = (turned - high.astype(F32)).astype(BF16)
-                split[h, k, pl.ds(0, half), pl.ds(t * block, block)] = high
-                split[h, k, pl.ds(half, half), pl.ds(t * block, block)] = low
-
-    lanes = min(256, states)
-    n_blocks = states // lanes
-    targets = lanes // (2 * share)
-    own_block = a // targets if targets > 1 else a
-
-    toward = 2 * ((2 * a) // n_ka) - 1
-
-    def block_of(s):
-        return lax.rem(own_block + toward * (1 + s) + n_blocks, n_blocks)
+                value = comb[h, v * block : (v + 1) * block, k * half : (k + 1) * half]
+                value = jnp.where(row_index + v * block < counts_ref[k], value, 0.0)
+                high = value.astype(BF16)
+                low = (value - high.astype(F32)).astype(BF16)
+                start = k * rows + v * block
+                split[h, start : start + block, 0:half] = high
+                split[h, start : start + block, half:] = low
+
+    targets = n_ka // parts
+    size = targets * share
+
+    toward = (2 * a) // n_ka
+
+    def part_of(s):
+        return lax.rem(toward + 1 + s, parts)
 
     def part_copy(h, s):
-        size = targets * share
-        span = pl.ds(pl.multiple_of(block_of(s) * size, size), size)
+        span = pl.ds(pl.multiple_of(part_of(s) * size, size), size)
         return pltpu.make_async_remote_copy(
             src_ref=amp.at[h, other, span],
             dst_ref=part.at[h, span],
@@ -226,6 +251,9 @@
             device_id={"vib": other},
             device_id_type=MESH,
         )
+
+    def target_of(s, j):
+        return part_of(s) * targets + (1 - toward) * (targets - 1 - j) + toward * j
 
     def out_copies(h, sender, target, slot):
         values = pltpu.make_async_remote_copy(
@@ -269,7 +297,7 @@
     def finish(h, s):
         part_copy(h, s).wait_recv()
         for j in range(targets):
-            target = block_of(s) * targets + j
+            target = target_of(s, j)
             span = pl.ds(pl.multiple_of(target * share, share), share)
             slot = s * targets + j
             value = amp[h, b, span, :] + part[h, span, :]
@@ -287,15 +315,14 @@
                     copy.start()
 
     def amplitude_block(h, s):
-        cols = pl.ds(pl.multiple_of(block_of(s) * lanes, lanes), lanes)
-        both = jnp.dot(split[h, 0], ini[0, :, cols], preferred_element_type=F32)
-        for k in range(1, kblocks):
-            both = both + jnp.dot(split[h, k], ini[k, :, cols], preferred_element_type=F32)
-        value = (both[:half] + both[half:]).T
+        lanes = states // parts
+        span = pl.ds(pl.multiple_of(part_of(s) * lanes, lanes), lanes)
+        both = jnp.dot(turned[span, :], split[h], preferred_element_type=F32)
+        value = both[:, :half] + both[:, half:]
         for j in range(targets):
             for core in range(2):
                 low = (j * 2 + core) * share
-                target = block_of(s) * targets + j
+                target = part_of(s) * targets + j
                 amp[h, core, pl.ds(pl.multiple_of(target * share, share), share), :] = value[
                     low : low + share
                 ]
@@ -317,21 +344,20 @@
             take(h, other, j)
         split_half(h)
         if h == 0:
-            get_initial.wait()
             for r in range(1, rounds + 1):
                 for side in range(2):
                     if r > 1:
                         token(side, r)
                 for side in range(2):
                     await_token(side, r)
-        for s in range(n_blocks):
+        for s in range(parts):
             amplitude_block(h, s)
             if s > 0:
                 finish(h, s - 1)
-            if s == n_blocks // 2 and h + 1 < n_half:
+            if s == 0 and h + 1 < n_half:
                 relay(h + 1, 0)
     for h in range(n_half):
-        finish(h, n_blocks - 1)
+        finish(h, parts - 1)
 
     for h in range(n_half):
         for d in range(1, n_ka):
@@ -343,8 +369,14 @@
                 zrecv[h, sender].astype(F32) * srecv[h, sender, 0:1, :]
             )
 
-    for h in range(n_half):
-        own_copy(h).wait_send()
+    for side in range(2):
+        @pl.when(sends[side])
+        def _():
+            count_copy(side).wait_send()
+
+    for h in range(n_half):
+        for k in range(kblocks):
+            own_copy(h, k).wait_send()
         for j in range(chunks):
             for side in range(2):
                 @pl.when(sends[side])
@@ -354,10 +386,10 @@
                 @pl.when(takes[side])
                 def _():
                     forward(side, h, j).wait_send()
-        for s in range(n_blocks):
+        for s in range(parts):
             part_copy(h, s).wait_send()
             for j in range(targets):
-                target = block_of(s) * targets + j
+                target = target_of(s, j)
 
                 @pl.when(target != a)
                 def _():
@@ -374,9 +406,9 @@
     half = width // n_half
     chunks = 2
     dma = pltpu.SemaphoreType.DMA
-    n_blocks = states // min(256, states)
+    parts = 2
     amplitude = pl.pallas_call(
-        functools.partial(kernel, n_ka, n_half, chunks),
+        functools.partial(kernel, n_ka, n_half, chunks, parts),
         out_shape=jax.ShapeDtypeStruct((share, width), F32),
         in_specs=[pl.BlockSpec(memory_space=pltpu.SMEM)]
         + [pl.BlockSpec(memory_space=pl.ANY)] * 3,
@@ -384,28 +416,32 @@
         scratch_shapes=[
             pltpu.VMEM(moments.shape, BF16),
             pltpu.VMEM(initial_vectors.shape, BF16),
-            pltpu.VMEM(final_vectors.shape, BF16),
+            pltpu.VMEM((states, kblocks * rows), BF16),
             pltpu.VMEM((n_half, whole, kblocks * half), BF16),
             pltpu.VMEM((n_half, whole, 2 * half), BF16),
             pltpu.VMEM((n_half, rows, kblocks * half), F32),
-            pltpu.VMEM((n_half, kblocks, 2 * half, rows), BF16),
+            pltpu.VMEM((n_half, kblocks * rows, 2 * half), BF16),
             pltpu.VMEM((n_half, 2, n_ka * share, half), F32),
             pltpu.VMEM((n_half, n_ka * share, half), F32),
             pltpu.VMEM((n_half, n_ka, share, half), jnp.int16),
             pltpu.VMEM((n_half, n_ka, share, half), jnp.int16),
             pltpu.VMEM((n_half, n_ka, 8, half), F32),
             pltpu.VMEM((n_half, n_ka, 8, half), F32),
+            pltpu.VMEM((2, 8, half), jnp.int32),
+            pltpu.VMEM((2, 8, half), jnp.int32),
             dma((2, 2)),
             dma(()),
-            dma((n_half, chunks)),
-            dma((n_half,)),
-            dma((n_half,)),
+            dma((n_half, kblocks)),
+            dma((n_half, kblocks)),
+            dma((n_half, kblocks)),
             dma((2, n_half, chunks)),
             dma((2, n_half, chunks)),
+            dma((2,)),
+            dma((2,)),
             dma((2, n_half, chunks)),
             dma((2, n_half, chunks)),
-            dma((n_half, n_blocks)),
-            dma((n_half, n_blocks)),
+            dma((n_half, parts)),
+            dma((n_half, parts)),
             dma((n_half, n_ka)),
             dma((n_half, n_ka)),
             dma((n_half, n_ka)),

time: 31 us -> 31.4 us (1.013)
  Pallas kernels: 29.1 us -> 29.5 us
    pallas_call x1, Pallas kernels: 29.1 us -> 29.5 us  [on_device(): pl.pallas_call(functools.partial(kernel, n_ka, n_half, chunks, parts), ou...]
where the time goes in v2:
time: 31.4 us; the launch traced here: 31.2 us
  Pallas kernels  29.5 us (94%)
  other arithmetic  1.65 us (5%)
    pallas_call x1, Pallas kernels, on_device(): pl.pallas_call(functools.partial(kernel, n_ka, n_half, chunks, parts), ou...  29.5 us
    mul x1, other arithmetic, on_device(): return amplitude * amplitude  1.65 us

profile of v2, /device:TPU:0, one launch (start us, length us, event | category | flops | bytes accessed | tf_op | source)
XLA Modules:
  0.0 31.2 jit_solution(14127221743236448000)
XLA Ops:
  0.0 29.5 %shard_map.46 = f32[128,256]{1,0:T(8,128)} custom-call(s32[2]{0:T(128)} %counts_ref.1, bf16[2,1024,2048]{2,1,0:T(8,128)(2,1)} %moments_hbm.1, bf16[2,1024,1024]{2,1,0:T(8,128)(2,1)} %initial_hbm.1, bf16[2,1024,256]{2,1,0:T(8,128)(2,1)} %final_hbm.1), custom_call_target="tpu_custom_call" | custom-call | tf_op jit(solution)/shard_map/pallas_call | solution.py:410
  29.6 1.7 %mul.3 = f32[128,256]{1,0:T(8,128)} multiply(f32[128,256]{1,0:T(8,128)} %shard_map.46, f32[128,256]{1,0:T(8,128)} %shard_map.46) | non-fusion elementwise | flops 32768 | bytes 393216 | tf_op jit(solution)/shard_map/mul | solution.py:456

commit v3 on v2

--- a/solution.py
+++ b/solution.py
@@ -42,6 +42,21 @@
     other = 1 - b
     first = a * kblocks - kblocks * n_ka // 2
 
+    has_up = a < n_ka - 1
+    has_down = a > 0
+    sends = (has_up, has_down)
+    takes = (has_down, has_up)
+    toward_side = (a + 1, a - 1)
+
+    barrier = pltpu.get_barrier_semaphore()
+    pl.semaphore_signal(barrier, inc=1, device_id={"vib": other}, device_id_type=MESH)
+    for side in range(2):
+        @pl.when(sends[side])
+        def _():
+            pl.semaphore_signal(
+                barrier, inc=1, device_id={"ka": toward_side[side]}, device_id_type=MESH
+            )
+
     step = rows // chunks
     last = kblocks - 1
     cores = (b, other)
@@ -70,22 +85,6 @@
         for c in range(2):
             get_moments(i, c).start()
     get_initial = pltpu.make_async_copy(initial_hbm, ini, ini_sem)
-    get_initial.start()
-
-    has_up = a < n_ka - 1
-    has_down = a > 0
-    sends = (has_up, has_down)
-    takes = (has_down, has_up)
-    toward_side = (a + 1, a - 1)
-
-    barrier = pltpu.get_barrier_semaphore()
-    pl.semaphore_signal(barrier, inc=1, device_id={"vib": other}, device_id_type=MESH)
-    for side in range(2):
-        @pl.when(sends[side])
-        def _():
-            pl.semaphore_signal(
-                barrier, inc=1, device_id={"ka": toward_side[side]}, device_id_type=MESH
-            )
 
     def at(core, j):
         return pl.ds(pl.multiple_of(core * rows + j * step, step), step)
@@ -162,6 +161,26 @@
     cross_row = jnp.concatenate([lower1, upper0], axis=1)
     edge_row = jnp.concatenate([upper_below, lower_above], axis=1)
 
+    def token(side, r):
+        to = toward_side[side]
+        sem = (token_up, token_down)[side]
+        about = a - 1 - r if side == 0 else a + 1 + r
+        known = about >= 0 if side == 0 else about <= n_ka - 1
+
+        @pl.when(jnp.logical_and(known, sends[side]))
+        def _():
+            pl.semaphore_signal(sem.at[r - 1], inc=1, device_id={"ka": to}, device_id_type=MESH)
+
+    def await_token(side, r):
+        sem = (token_up, token_down)[side]
+        told = a - 2 - r >= 0 if side == 0 else a + 2 + r <= n_ka - 1
+
+        @pl.when(told)
+        def _():
+            pl.semaphore_wait(sem.at[r - 1], 1)
+
+    rounds = max(0, n_ka - 3)
+
     def relay(h, j):
         for side in range(2):
             @pl.when(takes[side])
@@ -169,40 +188,59 @@
                 z_copy(side, h, j).wait_recv()
                 forward(side, h, j).start()
 
-    tile = rows // 2
+    tile = min(256, rows)
+
+    def own_piece(i, h):
+        row_index = lax.broadcasted_iota(jnp.int32, (rows, half), 0) + cores[i] * rows
+        masked = []
+        for k in range(kblocks):
+            if i == 0:
+                get_own(h, k).wait()
+            else:
+                own_copy(h, k).wait_recv()
+            piece = own[h, cols_of(cores[i]), half_lanes(k)].astype(F32)
+            masked.append(jnp.where(row_index < counts_ref[k], piece, 0.0).astype(BF16))
+        return jnp.concatenate(masked, axis=1)
+
+    def moments_ready(i):
+        for c in range(2):
+            get_moments(i, c).wait()
+
+    def own_half(i, h):
+        piece = own_piece(i, h)
+        if h == 0:
+            moments_ready(i)
+            if i == 0:
+                get_initial.start()
+        for t in range(rows // tile):
+            span = pl.ds(t * tile, tile)
+            along_z = jnp.dot(mom[0, span, cols_of(cores[i])], piece, preferred_element_type=F32)
+            along_x = jnp.dot(mom[1, span, cols_of(cores[i])], piece, preferred_element_type=F32)
+            crossed = jnp.concatenate([along_x[:, half:], along_x[:, :half]], axis=1)
+            value = same_row * along_z + cross_row * crossed
+            comb[h, span, :] = value if i == 0 else comb[h, span, :] + value
+
     for i in range(2):
-        row_index = lax.broadcasted_iota(jnp.int32, (rows, half), 0) + cores[i] * rows
         for h in range(n_half):
-            masked = []
-            for k in range(kblocks):
-                if i == 0:
-                    get_own(h, k).wait()
-                else:
-                    own_copy(h, k).wait_recv()
-                piece = own[h, cols_of(cores[i]), half_lanes(k)].astype(F32)
-                masked.append(jnp.where(row_index < counts_ref[k], piece, 0.0).astype(BF16))
-            piece = jnp.concatenate(masked, axis=1)
-            if h == 0:
-                for c in range(2):
-                    get_moments(i, c).wait()
-            for t in range(2):
-                span = pl.ds(t * tile, tile)
-                along_z = jnp.dot(
-                    mom[0, span, cols_of(cores[i])], piece, preferred_element_type=F32
-                )
-                along_x = jnp.dot(
-                    mom[1, span, cols_of(cores[i])], piece, preferred_element_type=F32
-                )
-                crossed = jnp.concatenate([along_x[:, half:], along_x[:, :half]], axis=1)
-                value = same_row * along_z + cross_row * crossed
-                comb[h, span, :] = value if i == 0 else comb[h, span, :] + value
-
-    get_initial.wait()
+            own_half(i, h)
+
+    early = (chunks + 1) // 2
+    for j in range(early):
+        relay(0, j)
+    if rounds > 0:
+        for side in range(2):
+            token(side, 1)
+
     block = min(256, rows)
-    for k in range(kblocks):
-        for v in range(rows // block):
-            low = k * rows + v * block
-            turned[:, low : low + block] = ini[k, v * block : (v + 1) * block, :].T
+
+    def turn_initial():
+        get_initial.wait()
+        for k in range(kblocks):
+            for v in range(rows // block):
+                low = k * rows + v * block
+                turned[:, low : low + block] = ini[k, v * block : (v + 1) * block, :].T
+
+    turn_initial()
 
     for side in range(2):
         @pl.when(takes[side])
@@ -214,7 +252,7 @@
     def take(h, core, j):
         live = edge_index + (core * rows + j * step) < edge_counts
         piece = jnp.where(live, edge[h, at(core, j), :].astype(F32), 0.0).astype(BF16)
-        for t in range(2):
+        for t in range(rows // tile):
             span = pl.ds(t * tile, tile)
             comb[h, span, :] = comb[h, span, :] + edge_row * jnp.dot(
                 mom[1, span, at(core, j)], piece, preferred_element_type=F32
@@ -236,13 +274,8 @@
     targets = n_ka // parts
     size = targets * share
 
-    toward = (2 * a) // n_ka
-
-    def part_of(s):
-        return lax.rem(toward + 1 + s, parts)
-
     def part_copy(h, s):
-        span = pl.ds(pl.multiple_of(part_of(s) * size, size), size)
+        span = pl.ds(s * size, size)
         return pltpu.make_async_remote_copy(
             src_ref=amp.at[h, other, span],
             dst_ref=part.at[h, span],
@@ -251,9 +284,6 @@
             device_id={"vib": other},
             device_id_type=MESH,
         )
-
-    def target_of(s, j):
-        return part_of(s) * targets + (1 - toward) * (targets - 1 - j) + toward * j
 
     def out_copies(h, sender, target, slot):
         values = pltpu.make_async_remote_copy(
@@ -274,32 +304,11 @@
         )
         return values, scales
 
-    def token(side, r):
-        to = toward_side[side]
-        sem = (token_up, token_down)[side]
-        about = a - 1 - r if side == 0 else a + 1 + r
-        known = about >= 0 if side == 0 else about <= n_ka - 1
-
-        @pl.when(jnp.logical_and(known, sends[side]))
-        def _():
-            pl.semaphore_signal(sem.at[r - 1], inc=1, device_id={"ka": to}, device_id_type=MESH)
-
-    def await_token(side, r):
-        sem = (token_up, token_down)[side]
-        told = a - 2 - r >= 0 if side == 0 else a + 2 + r <= n_ka - 1
-
-        @pl.when(told)
-        def _():
-            pl.semaphore_wait(sem.at[r - 1], 1)
-
-    rounds = max(0, n_ka - 3)
-
     def finish(h, s):
         part_copy(h, s).wait_recv()
         for j in range(targets):
-            target = target_of(s, j)
-            span = pl.ds(pl.multiple_of(target * share, share), share)
-            slot = s * targets + j
+            target = s * targets + j
+            span = pl.ds(target * share, share)
             value = amp[h, b, span, :] + part[h, span, :]
 
             @pl.when(target == a)
@@ -309,39 +318,41 @@
             @pl.when(target != a)
             def _():
                 peak = jnp.maximum(jnp.max(jnp.abs(value), axis=0, keepdims=True), TINY)
-                zsend[h, slot] = jnp.round(value * (LEVELS / peak)).astype(jnp.int16)
-                ssend[h, slot] = jnp.broadcast_to(peak / LEVELS, (8, half))
-                for copy in out_copies(h, a, target, slot):
+                zsend[h, target] = jnp.round(value * (LEVELS / peak)).astype(jnp.int16)
+                ssend[h, target] = jnp.broadcast_to(peak / LEVELS, (8, half))
+                for copy in out_copies(h, a, target, target):
                     copy.start()
 
     def amplitude_block(h, s):
         lanes = states // parts
-        span = pl.ds(pl.multiple_of(part_of(s) * lanes, lanes), lanes)
-        both = jnp.dot(turned[span, :], split[h], preferred_element_type=F32)
-        value = both[:, :half] + both[:, half:]
-        for j in range(targets):
-            for core in range(2):
-                low = (j * 2 + core) * share
-                target = part_of(s) * targets + j
-                amp[h, core, pl.ds(pl.multiple_of(target * share, share), share), :] = value[
-                    low : low + share
+        for q in range(lanes // tile):
+            low = s * lanes + q * tile
+            both = jnp.dot(turned[low : low + tile, :], split[h], preferred_element_type=F32)
+            value = both[:, :half] + both[:, half:]
+            for piece in range(tile // share):
+                target, core = divmod(low // share + piece, 2)
+                amp[h, core, pl.ds(target * share, share), :] = value[
+                    piece * share : (piece + 1) * share
                 ]
         part_copy(h, s).start()
 
+    def take_other(h, j):
+        for side in range(2):
+            @pl.when(takes[side])
+            def _():
+                forward(side, h, j).wait_recv()
+        take(h, other, j)
+
     for h in range(n_half):
         for j in range(chunks):
-            if h == 0 or j > 0:
+            if h > 0 or j >= early:
                 relay(h, j)
-            if h + j == 0 and rounds > 0:
-                for side in range(2):
-                    token(side, 1)
             take(h, b, j)
-        for j in range(chunks):
-            for side in range(2):
-                @pl.when(takes[side])
-                def _():
-                    forward(side, h, j).wait_recv()
-            take(h, other, j)
+            if h > 0 and j == 0:
+                finish(h - 1, parts - 1)
+            if j > 0:
+                take_other(h, j - 1)
+        take_other(h, chunks - 1)
         split_half(h)
         if h == 0:
             for r in range(1, rounds + 1):
@@ -352,49 +363,53 @@
                     await_token(side, r)
         for s in range(parts):
             amplitude_block(h, s)
-            if s > 0:
-                finish(h, s - 1)
-            if s == 0 and h + 1 < n_half:
-                relay(h + 1, 0)
-    for h in range(n_half):
-        finish(h, parts - 1)
+        for s in range(parts - 1):
+            finish(h, s)
+    finish(n_half - 1, parts - 1)
+
+    def add_sums(h, d):
+        sender = lax.rem(a + d, n_ka)
+        for copy in out_copies(h, sender, sender, 0):
+            copy.wait_recv()
+        lanes_h = half_lanes(h)
+        out_ref[:, lanes_h] = out_ref[:, lanes_h] + (
+            zrecv[h, sender].astype(F32) * srecv[h, sender, 0:1, :]
+        )
 
     for h in range(n_half):
         for d in range(1, n_ka):
-            sender = lax.rem(a + d, n_ka)
-            for copy in out_copies(h, sender, sender, 0):
-                copy.wait_recv()
-            lanes_h = pl.ds(h * half, half)
-            out_ref[:, lanes_h] = out_ref[:, lanes_h] + (
-                zrecv[h, sender].astype(F32) * srecv[h, sender, 0:1, :]
-            )
-
-    for side in range(2):
-        @pl.when(sends[side])
-        def _():
-            count_copy(side).wait_send()
-
-    for h in range(n_half):
-        for k in range(kblocks):
-            own_copy(h, k).wait_send()
-        for j in range(chunks):
-            for side in range(2):
-                @pl.when(sends[side])
-                def _():
-                    z_copy(side, h, j).wait_send()
-
-                @pl.when(takes[side])
-                def _():
-                    forward(side, h, j).wait_send()
-        for s in range(parts):
-            part_copy(h, s).wait_send()
-            for j in range(targets):
-                target = target_of(s, j)
-
-                @pl.when(target != a)
-                def _():
-                    for copy in out_copies(h, a, target, s * targets + j):
-                        copy.wait_send()
+            add_sums(h, d)
+
+    def drain():
+        for side in range(2):
+            @pl.when(sends[side])
+            def _():
+                count_copy(side).wait_send()
+
+        for h in range(n_half):
+            for k in range(kblocks):
+                own_copy(h, k).wait_send()
+            for j in range(chunks):
+                for side in range(2):
+                    @pl.when(sends[side])
+                    def _():
+                        z_copy(side, h, j).wait_send()
+
+                    @pl.when(takes[side])
+                    def _():
+                        forward(side, h, j).wait_send()
+            for s in range(parts):
+                part_copy(h, s).wait_send()
+                for j in range(targets):
+                    target = s * targets + j
+
+                    @pl.when(target != a)
+                    def _():
+                        for copy in out_copies(h, a, target, target):
+                            copy.wait_send()
+
+
+    drain()
 
 
 def on_device(n_ka, moments, initial_vectors, final_vectors, basis_counts):
@@ -409,7 +424,7 @@
     parts = 2
     amplitude = pl.pallas_call(
         functools.partial(kernel, n_ka, n_half, chunks, parts),
-        out_shape=jax.ShapeDtypeStruct((share, width), F32),
+        out_shape=pltpu.VMEM((share, width), F32),
         in_specs=[pl.BlockSpec(memory_space=pltpu.SMEM)]
         + [pl.BlockSpec(memory_space=pl.ANY)] * 3,
         out_specs=pl.BlockSpec(memory_space=pltpu.VMEM),

time: 31.4 us -> 28 us (0.89)
  Pallas kernels: 29.5 us -> 27.1 us
  other arithmetic: 1.65 us -> 0.67 us
    pallas_call x1, Pallas kernels: 29.5 us -> 27.1 us  [on_device(): pl.pallas_call(functools.partial(kernel, n_ka, n_half, chunks, parts), ou...]
    mul x1, other arithmetic: 1.65 us -> 0.67 us  [on_device(): return amplitude * amplitude]
where the time goes in v3:
time: 28 us; the launch traced here: 27.8 us
  Pallas kernels  27.1 us (97%)
  other arithmetic  0.67 us (2%)
    pallas_call x1, Pallas kernels, on_device(): pl.pallas_call(functools.partial(kernel, n_ka, n_half, chunks, parts), ou...  27.1 us
    mul x1, other arithmetic, on_device(): return amplitude * amplitude  0.67 us

profile of v3, /device:TPU:0, one launch (start us, length us, event | category | flops | bytes accessed | tf_op | source)
XLA Modules:
  0.0 27.8 jit_solution(3067319389454714334)
XLA Ops:
  0.0 27.1 %shard_map.46 = f32[128,256]{1,0:T(8,128)S(1)} custom-call(s32[2]{0:T(128)} %counts_ref.1, bf16[2,1024,2048]{2,1,0:T(8,128)(2,1)} %moments_hbm.1, bf16[2,1024,1024]{2,1,0:T(8,128)(2,1)} %initial_hbm.1, bf16[2,1024,256]{2,1,0:T(8,128)(2,1)} %final_hbm.1), custom_call_target="tpu_custom_call" | custom-call | tf_op jit(solution)/shard_map/pallas_call | solution.py:425
  27.1 0.7 %mul.3 = f32[128,256]{1,0:T(8,128)} multiply(f32[128,256]{1,0:T(8,128)S(1)} %shard_map.46, f32[128,256]{1,0:T(8,128)S(1)} %shard_map.46) | non-fusion elementwise | flops 32768 | bytes 393216 | tf_op jit(solution)/shard_map/mul | solution.py:471

commit v4 on v3

v4 whole, which is shorter than its diff:
```python
import functools

import jax
import jax.numpy as jnp
from jax import lax
from jax.experimental import pallas as pl
from jax.experimental.pallas import tpu as pltpu
from jax.sharding import PartitionSpec as P

JQ = 30
MESH = pl.DeviceIdType.MESH
F32 = jnp.float32
BF16 = jnp.bfloat16
LEVELS = 32767.0
TINY = 1e-30


def coefficient_rows(index, width):
    value = jnp.full((1, width), index, jnp.int32).astype(F32)
    jsquare = float(JQ * (JQ + 1))
    norm_j = jnp.sqrt(jnp.full((1, width), jsquare, F32))
    same = value / norm_j
    upper = 0.5 * jnp.sqrt(jsquare - value * (value + 1.0)) / norm_j
    lower = -0.5 * jnp.sqrt(jsquare - value * (value - 1.0)) / norm_j
    return same, upper, lower


def kernel(
    n_ka, n_half, chunks, groups, counts_hbm, moments_hbm, initial_hbm, final_hbm, out_ref,
    counts, mom, ini, turned, own, edge, comb, split, away, part, zsend, zrecv, ssend, srecv, csend, crecv,
    counts_sem, mom_sem, ini_sem, own_sem, own_send, own_recv, z_send, z_recv, count_send, count_recv,
    fwd_send, fwd_recv, part_send, part_recv, out_send, out_recv, scale_send, scale_recv,
    token_up, token_down,
):
    kblocks, rows, states = ini.shape
    width = final_hbm.shape[2]
    share = out_ref.shape[0]
    whole = mom.shape[2]
    half = width // n_half
    step = rows // chunks
    last = kblocks - 1
    tile = min(256, rows)
    a = lax.axis_index("ka")
    b = lax.axis_index("vib")
    other = 1 - b
    first = a * kblocks - kblocks * n_ka // 2
    cores = (b, other)
    has_up = a < n_ka - 1
    has_down = a > 0
    sends = (has_up, has_down)
    takes = (has_down, has_up)
    toward_side = (a + 1, a - 1)

    barrier = pltpu.get_barrier_semaphore()
    pl.semaphore_signal(barrier, inc=1, device_id={"vib": other}, device_id_type=MESH)
    for side in range(2):
        @pl.when(sends[side])
        def _():
            pl.semaphore_signal(
                barrier, inc=1, device_id={"ka": toward_side[side]}, device_id_type=MESH
            )

    def rows_of(core):
        return pl.ds(pl.multiple_of(core * rows, rows), rows)

    def at(core, j):
        return pl.ds(pl.multiple_of(core * rows + j * step, step), step)

    def half_lanes(i):
        return pl.ds(i * half, half)

    def get_own(h):
        return pltpu.make_async_copy(
            final_hbm.at[:, :, half_lanes(h)], own.at[h, :, rows_of(b)], own_sem.at[h]
        )

    def get_moments(i):
        span = rows_of(cores[i])
        return pltpu.make_async_copy(moments_hbm.at[:, :, span], mom.at[:, :, span], mom_sem.at[i])

    get_counts = pltpu.make_async_copy(counts_hbm, counts, counts_sem)
    get_initial = pltpu.make_async_copy(initial_hbm, ini, ini_sem)

    def own_copy(h):
        return pltpu.make_async_remote_copy(
            src_ref=final_hbm.at[:, :, half_lanes(h)],
            dst_ref=own.at[h, :, rows_of(b)],
            send_sem=own_send.at[h],
            recv_sem=own_recv.at[h],
            device_id={"vib": other},
            device_id_type=MESH,
        )

    def z_copy(side, h, j):
        return pltpu.make_async_remote_copy(
            src_ref=final_hbm.at[last * (1 - side), pl.ds(j * step, step), half_lanes(h)],
            dst_ref=edge.at[h, at(b, j), half_lanes(side)],
            send_sem=z_send.at[side],
            recv_sem=z_recv.at[side, h, j],
            device_id={"ka": toward_side[side]},
            device_id_type=MESH,
        )

    def count_copy(side):
        return pltpu.make_async_remote_copy(
            src_ref=csend.at[side],
            dst_ref=crecv.at[side],
            send_sem=count_send.at[side],
            recv_sem=count_recv.at[side],
            device_id={"ka": toward_side[side]},
            device_id_type=MESH,
        )

    def forward(h, j):
        return pltpu.make_async_remote_copy(
            src_ref=edge.at[h, at(b, j)],
            dst_ref=edge.at[h, at(b, j)],
            send_sem=fwd_send,
            recv_sem=fwd_recv.at[h, j],
            device_id={"vib": other},
            device_id_type=MESH,
        )

    def start_edges(h):
        for j in range(chunks):
            for side in range(2):
                @pl.when(sends[side])
                def _():
                    z_copy(side, h, j).start()

    def start_loads():
        get_counts.start()
        for h in range(n_half):
            get_own(h).start()
        for i in range(2):
            get_moments(i).start()

    def greet():
        for side in range(2):
            @pl.when(jnp.logical_not(takes[side]))
            def _():
                crecv[side] = jnp.zeros(crecv.shape[1:], jnp.int32)
                for h in range(n_half):
                    edge[h, rows_of(b), side * half : (side + 1) * half] = jnp.zeros((rows, half), BF16)
        get_counts.wait()
        for side in range(2):
            csend[side] = jnp.full(csend.shape[1:], counts[last * (1 - side)], jnp.int32)
        pl.semaphore_wait(barrier, 1 + has_up.astype(jnp.int32) + has_down.astype(jnp.int32))
        for side in range(2):
            @pl.when(sends[side])
            def _():
                count_copy(side).start()
        start_edges(0)
        for h in range(n_half):
            own_copy(h).start()

    start_loads()
    greet()

    same0, upper0, _ = coefficient_rows(first, half)
    same1, _, lower1 = coefficient_rows(first + 1, half)
    _, upper_below, _ = coefficient_rows(first - 1, half)
    _, _, lower_above = coefficient_rows(first + 2, half)
    same_row = jnp.concatenate([same0, same1], axis=1)
    cross_row = jnp.concatenate([lower1, upper0], axis=1)
    edge_row = jnp.concatenate([upper_below, lower_above], axis=1)

    rounds = max(0, n_ka - 3)

    def token(side, r):
        sem = (token_up, token_down)[side]
        known = a - 1 - r >= 0 if side == 0 else a + 1 + r <= n_ka - 1

        @pl.when(jnp.logical_and(known, sends[side]))
        def _():
            pl.semaphore_signal(
                sem.at[r - 1], inc=1, device_id={"ka": toward_side[side]}, device_id_type=MESH
            )

    def await_token(side, r):
        sem = (token_up, token_down)[side]

        @pl.when(a - 2 - r >= 0 if side == 0 else a + 2 + r <= n_ka - 1)
        def _():
            pl.semaphore_wait(sem.at[r - 1], 1)

    def relay(h, j):
        for side in range(2):
            @pl.when(takes[side])
            def _():
                z_copy(side, h, j).wait_recv()
        forward(h, j).start()

    def own_half(i, h):
        row_index = lax.broadcasted_iota(jnp.int32, (rows, half), 0) + cores[i] * rows
        if i == 0:
            get_own(h).wait()
        else:
            own_copy(h).wait_recv()
        masked = []
        for k in range(kblocks):
            piece = own[h, k, rows_of(cores[i]), :].astype(F32)
            masked.append(jnp.where(row_index < counts[k], piece, 0.0).astype(BF16))
        piece = jnp.concatenate(masked, axis=1)
        if h == 0:
            get_moments(i).wait()
            if i == 0:
                get_initial.start()
        for t in range(rows // tile):
            span = pl.ds(t * tile, tile)
            along_z = jnp.dot(mom[0, span, rows_of(cores[i])], piece, preferred_element_type=F32)
            along_x = jnp.dot(mom[1, span, rows_of(cores[i])], piece, preferred_element_type=F32)
            crossed = jnp.concatenate([along_x[:, half:], along_x[:, :half]], axis=1)
            value = same_row * along_z + cross_row * crossed
            comb[h, span, :] = value if i == 0 else comb[h, span, :] + value

    def turn_initial():
        get_initial.wait()
        for k in range(kblocks):
            for v in range(rows // tile):
                block = ini[k, v * tile : (v + 1) * tile, :].T
                low = k * rows + v * tile
                for target in range(n_ka):
                    for core in range(2):
                        start = (target * 2 + core) * share
                        turned[core, target * share : (target + 1) * share, low : low + tile] = block[
                            start : start + share
                        ]

    row_index = lax.broadcasted_iota(jnp.int32, (tile, half), 0) + b * rows

    def take(h, core, low, size, last_take=False):
        start = core * rows + low
        edge_index = lax.broadcasted_iota(jnp.int32, (size, 2 * half), 0)
        edge_counts = jnp.concatenate([crecv[0, 0:1, :], crecv[1, 0:1, :]], axis=1)
        span_w = pl.ds(pl.multiple_of(start, size), size)
        piece = edge[h, span_w, :].astype(F32)
        piece = jnp.where(edge_index + start < edge_counts, piece, 0.0).astype(BF16)
        for t in range(rows // tile):
            span = pl.ds(t * tile, tile)
            value = comb[h, span, :] + edge_row * jnp.dot(
                mom[1, span, span_w], piece, preferred_element_type=F32
            )
            if not last_take:
                comb[h, span, :] = value
                continue
            for k in range(kblocks):
                live = jnp.where(
                    row_index + t * tile < counts[k], value[:, k * half : (k + 1) * half], 0.0
                )
                high = live.astype(BF16)
                start_v = k * rows + t * tile
                split[h, start_v : start_v + tile, 0:half] = high
                split[h, start_v : start_v + tile, half:] = (live - high.astype(F32)).astype(BF16)

    targets = n_ka // groups
    size = targets * share

    def part_copy(h, g):
        return pltpu.make_async_remote_copy(
            src_ref=away.at[h, pl.ds(g * size, size)],
            dst_ref=part.at[h, pl.ds(g * size, size)],
            send_sem=part_send,
            recv_sem=part_recv.at[h, g],
            device_id={"vib": other},
            device_id_type=MESH,
        )

    def out_copies(h, sender, target):
        values = pltpu.make_async_remote_copy(
            src_ref=zsend.at[h, target],
            dst_ref=zrecv.at[h, sender],
            send_sem=out_send,
            recv_sem=out_recv.at[h],
            device_id={"ka": target},
            device_id_type=MESH,
        )
        scales = pltpu.make_async_remote_copy(
            src_ref=ssend.at[h, target],
            dst_ref=srecv.at[h, sender],
            send_sem=scale_send,
            recv_sem=scale_recv.at[h],
            device_id={"ka": target},
            device_id_type=MESH,
        )
        return values, scales

    def amplitude(h, core, g):
        both = jnp.dot(
            turned[core, g * size : (g + 1) * size, :], split[h], preferred_element_type=F32
        )
        return both[:, :half] + both[:, half:]

    def send_away(h, g):
        away[h, g * size : (g + 1) * size, :] = amplitude(h, other, g)
        part_copy(h, g).start()

    def finish(h, g):
        mine = amplitude(h, b, g)
        part_copy(h, g).wait_recv()
        mine = mine + part[h, g * size : (g + 1) * size, :]
        for j in range(targets):
            target = g * targets + j
            value = mine[j * share : (j + 1) * share]

            @pl.when(target == a)
            def _():
                out_ref[:, half_lanes(h)] = value

            @pl.when(target != a)
            def _():
                peak = jnp.maximum(jnp.max(jnp.abs(value), axis=0, keepdims=True), TINY)
                zsend[h, target] = jnp.round(value * (LEVELS / peak)).astype(jnp.int16)
                ssend[h, target] = jnp.broadcast_to(peak / LEVELS, (8, half))
                for copy in out_copies(h, a, target):
                    copy.start()

    def all_out(ref, h, send_sem, recv_sem):
        span = ref.at[h, pl.ds(0, n_ka - 1)]
        return pltpu.make_async_remote_copy(
            src_ref=span, dst_ref=span, send_sem=send_sem, recv_sem=recv_sem,
            device_id={"vib": other}, device_id_type=MESH,
        )

    def add_sums(h):
        all_out(zrecv, h, out_send, out_recv.at[h]).wait_recv()
        all_out(srecv, h, scale_send, scale_recv.at[h]).wait_recv()
        total = out_ref[:, half_lanes(h)]
        for d in range(1, n_ka):
            sender = lax.rem(a + d, n_ka)
            total = total + zrecv[h, sender].astype(F32) * srecv[h, sender, 0:1, :]
        out_ref[:, half_lanes(h)] = total

    own_half(0, 0)
    if n_half > 1:
        own_half(0, 1)
    own_half(1, 0)
    for h in range(1, n_half):
        start_edges(h)
    if n_half > 1:
        own_half(1, 1)
    for j in range(chunks):
        if j > 0 or chunks == 1:
            turn_initial()
        relay(0, j)
        if j == 0 and rounds > 0:
            for side in range(2):
                token(side, 1)
    for side in range(2):
        @pl.when(takes[side])
        def _():
            count_copy(side).wait_recv()
    for h in range(n_half):
        if h == 0:
            take(h, b, 0, rows)
            for j in range(chunks):
                forward(h, j).wait_recv()
            take(h, other, 0, rows, last_take=True)
            for r in range(1, rounds + 1):
                for side in range(2):
                    if r > 1:
                        token(side, r)
                for side in range(2):
                    await_token(side, r)
        else:
            for j in range(chunks):
                relay(h, j)
                take(h, b, j * step, step)
                if j > 0:
                    forward(h, j - 1).wait_recv()
                    take(h, other, (j - 1) * step, step)
            forward(h, chunks - 1).wait_recv()
            take(h, other, rows - step, step, last_take=True)
        for g in range(groups):
            send_away(h, g)
        for g in range(groups):
            finish(h, g)
    for h in range(n_half):
        add_sums(h)

    def drain():
        for side in range(2):
            @pl.when(sends[side])
            def _():
                count_copy(side).wait_send()
                pltpu.make_async_remote_copy(
                    src_ref=final_hbm.at[0], dst_ref=final_hbm.at[0],
                    send_sem=z_send.at[side], recv_sem=z_recv.at[side, 0, 0],
                    device_id={"vib": other}, device_id_type=MESH,
                ).wait_send()
        for h in range(n_half):
            own_copy(h).wait_send()
            all_out(zsend, h, out_send, out_recv.at[h]).wait_send()
            all_out(ssend, h, scale_send, scale_recv.at[h]).wait_send()
        for buffer, sem in ((edge.at[:, rows_of(b)], fwd_send), (away, part_send)):
            pltpu.make_async_remote_copy(
                src_ref=buffer, dst_ref=buffer, send_sem=sem, recv_sem=sem,
                device_id={"vib": other}, device_id_type=MESH,
            ).wait_send()

    drain()


def on_device(n_ka, moments, initial_vectors, final_vectors, basis_counts):
    kblocks, rows, states = initial_vectors.shape
    width = final_vectors.shape[2]
    whole = moments.shape[2]
    share = states // (2 * n_ka)
    n_half = max(1, width // 128)
    half = width // n_half
    chunks = 2
    groups = 2
    dma = pltpu.SemaphoreType.DMA
    vmem = pltpu.VMEM
    amplitude = pl.pallas_call(
        functools.partial(kernel, n_ka, n_half, chunks, groups),
        out_shape=vmem((share, width), F32),
        in_specs=[pl.BlockSpec(memory_space=pl.ANY)] * 4,
        out_specs=pl.BlockSpec(memory_space=pltpu.VMEM),
        scratch_shapes=[
            pltpu.SMEM((kblocks,), jnp.int32),
            vmem(moments.shape, BF16),
            vmem(initial_vectors.shape, BF16),
            vmem((2, n_ka * share, kblocks * rows), BF16),
            vmem((n_half, kblocks, whole, half), BF16),
            vmem((n_half, whole, 2 * half), BF16),
            vmem((n_half, rows, kblocks * half), F32),
            vmem((n_half, kblocks * rows, 2 * half), BF16),
            vmem((n_half, n_ka * share, half), F32),
            vmem((n_half, n_ka * share, half), F32),
            vmem((n_half, n_ka, share, half), jnp.int16),
            vmem((n_half, n_ka, share, half), jnp.int16),
            vmem((n_half, n_ka, 8, half), F32),
            vmem((n_half, n_ka, 8, half), F32),
            vmem((2, 8, half), jnp.int32),
            vmem((2, 8, half), jnp.int32),
            dma(()),
            dma((2,)),
            dma(()),
            dma((n_half,)),
            dma((n_half,)),
            dma((n_half,)),
            dma((2,)),
            dma((2, n_half, chunks)),
            dma((2,)),
            dma((2,)),
            dma(()),
            dma((n_half, chunks)),
            dma(()),
            dma((n_half, groups)),
            dma(()),
            dma((n_half,)),
            dma(()),
            dma((n_half,)),
            pltpu.SemaphoreType.REGULAR((max(1, n_ka - 3),)),
            pltpu.SemaphoreType.REGULAR((max(1, n_ka - 3),)),
        ],
        compiler_params=pltpu.CompilerParams(
            collective_id=0, has_side_effects=True, vmem_limit_bytes=60 * 2**20
        ),
    )(basis_counts, moments, initial_vectors, final_vectors)
    return amplitude * amplitude


def solution(mesh):
    in_specs = (
        P(None, "vib", None),
        P("ka", "vib", "grp"),
        P("ka", "vib", ("grp", "fin")),
        P(("grp", "ka")),
    )
    out_specs = P(("grp", "ka", "vib"), "fin")
    return jax.shard_map(
        functools.partial(on_device, mesh.shape["ka"]),
        mesh=mesh, in_specs=in_specs, out_specs=out_specs, check_vma=False,
    )
```

time: 28 us -> 27.5 us (0.982)
  Pallas kernels: 27.1 us -> 26.7 us
    pallas_call x1, Pallas kernels: 27.1 us -> 26.7 us  [on_device(): pl.pallas_call(functools.partial(kernel, n_ka, n_half, chunks, groups), o...]
where the time goes in v4:
time: 27.5 us; the launch traced here: 27.3 us
  Pallas kernels  26.7 us (97%)
  other arithmetic  0.67 us (2%)
    pallas_call x1, Pallas kernels, on_device(): pl.pallas_call(functools.partial(kernel, n_ka, n_half, chunks, groups), o...  26.7 us
    mul x1, other arithmetic, on_device(): return amplitude * amplitude  0.67 us

profile of v4, /device:TPU:0, one launch (start us, length us, event | category | flops | bytes accessed | tf_op | source)
XLA Modules:
  0.0 27.3 jit_solution(17132206250536349183)
XLA Ops:
  0.0 26.7 %shard_map.46 = f32[128,256]{1,0:T(8,128)S(1)} custom-call(s32[2]{0:T(128)} %counts_hbm.1, bf16[2,1024,2048]{2,1,0:T(8,128)(2,1)} %moments_hbm.1, bf16[2,1024,1024]{2,1,0:T(8,128)(2,1)} %initial_hbm.1, bf16[2,1024,256]{2,1,0:T(8,128)(2,1)} %final_hbm.1), custom_call_target="tpu_custom_call" | custom-call | tf_op jit(solution)/shard_map/pallas_call | solution.py:415
  26.7 0.7 %mul.3 = f32[128,256]{1,0:T(8,128)} multiply(f32[128,256]{1,0:T(8,128)S(1)} %shard_map.46, f32[128,256]{1,0:T(8,128)S(1)} %shard_map.46) | non-fusion elementwise | flops 32768 | bytes 393216 | tf_op jit(solution)/shard_map/mul | solution.py:462

commit v5 on v4

--- a/solution.py
+++ b/solution.py
@@ -1,4 +1,5 @@
 import functools
+import math
 
 import jax
 import jax.numpy as jnp
@@ -26,8 +27,8 @@
 
 
 def kernel(
-    n_ka, n_half, chunks, groups, counts_hbm, moments_hbm, initial_hbm, final_hbm, out_ref,
-    counts, mom, ini, turned, own, edge, comb, split, away, part, zsend, zrecv, ssend, srecv, csend, crecv,
+    n_ka, n_half, cuts, groups, counts_hbm, moments_hbm, initial_hbm, final_hbm, out_ref,
+    counts, mom, ini, turned, own, edge, comb, split, away, mine, part, zsend, zrecv, ssend, srecv, csend, crecv,
     counts_sem, mom_sem, ini_sem, own_sem, own_send, own_recv, z_send, z_recv, count_send, count_recv,
     fwd_send, fwd_recv, part_send, part_recv, out_send, out_recv, scale_send, scale_recv,
     token_up, token_down,
@@ -37,7 +38,6 @@
     share = out_ref.shape[0]
     whole = mom.shape[2]
     half = width // n_half
-    step = rows // chunks
     last = kblocks - 1
     tile = min(256, rows)
     a = lax.axis_index("ka")
@@ -63,8 +63,16 @@
     def rows_of(core):
         return pl.ds(pl.multiple_of(core * rows, rows), rows)
 
-    def at(core, j):
-        return pl.ds(pl.multiple_of(core * rows + j * step, step), step)
+    def chunk(h, j):
+        bounds = cuts[h]
+        return bounds[j], bounds[j + 1] - bounds[j]
+
+    def chunks(h):
+        return range(len(cuts[h]) - 1)
+
+    def at(core, h, j):
+        low, count = chunk(h, j)
+        return pl.ds(pl.multiple_of(core * rows + low, math.gcd(rows, low)), count)
 
     def half_lanes(i):
         return pl.ds(i * half, half)
@@ -93,8 +101,8 @@
 
     def z_copy(side, h, j):
         return pltpu.make_async_remote_copy(
-            src_ref=final_hbm.at[last * (1 - side), pl.ds(j * step, step), half_lanes(h)],
-            dst_ref=edge.at[h, at(b, j), half_lanes(side)],
+            src_ref=final_hbm.at[last * (1 - side), pl.ds(*chunk(h, j)), half_lanes(h)],
+            dst_ref=edge.at[h, at(b, h, j), half_lanes(side)],
             send_sem=z_send.at[side],
             recv_sem=z_recv.at[side, h, j],
             device_id={"ka": toward_side[side]},
@@ -113,8 +121,8 @@
 
     def forward(h, j):
         return pltpu.make_async_remote_copy(
-            src_ref=edge.at[h, at(b, j)],
-            dst_ref=edge.at[h, at(b, j)],
+            src_ref=edge.at[h, at(b, h, j)],
+            dst_ref=edge.at[h, at(b, h, j)],
             send_sem=fwd_send,
             recv_sem=fwd_recv.at[h, j],
             device_id={"vib": other},
@@ -122,7 +130,7 @@
         )
 
     def start_edges(h):
-        for j in range(chunks):
+        for j in chunks(h):
             for side in range(2):
                 @pl.when(sends[side])
                 def _():
@@ -150,7 +158,8 @@
             @pl.when(sends[side])
             def _():
                 count_copy(side).start()
-        start_edges(0)
+        for h in range(n_half):
+            start_edges(h)
         for h in range(n_half):
             own_copy(h).start()
 
@@ -233,7 +242,7 @@
         start = core * rows + low
         edge_index = lax.broadcasted_iota(jnp.int32, (size, 2 * half), 0)
         edge_counts = jnp.concatenate([crecv[0, 0:1, :], crecv[1, 0:1, :]], axis=1)
-        span_w = pl.ds(pl.multiple_of(start, size), size)
+        span_w = pl.ds(pl.multiple_of(start, math.gcd(rows, low)), size)
         piece = edge[h, span_w, :].astype(F32)
         piece = jnp.where(edge_index + start < edge_counts, piece, 0.0).astype(BF16)
         for t in range(rows // tile):
@@ -253,6 +262,10 @@
                 split[h, start_v : start_v + tile, 0:half] = high
                 split[h, start_v : start_v + tile, half:] = (live - high.astype(F32)).astype(BF16)
 
+    def take_other(h, j):
+        forward(h, j).wait_recv()
+        take(h, other, *chunk(h, j), last_take=j == len(cuts[h]) - 2)
+
     targets = n_ka // groups
     size = targets * share
 
@@ -285,23 +298,34 @@
         )
         return values, scales
 
-    def amplitude(h, core, g):
-        both = jnp.dot(
-            turned[core, g * size : (g + 1) * size, :], split[h], preferred_element_type=F32
-        )
-        return both[:, :half] + both[:, half:]
-
-    def send_away(h, g):
-        away[h, g * size : (g + 1) * size, :] = amplitude(h, other, g)
-        part_copy(h, g).start()
-
-    def finish(h, g):
-        mine = amplitude(h, b, g)
-        part_copy(h, g).wait_recv()
-        mine = mine + part[h, g * size : (g + 1) * size, :]
-        for j in range(targets):
-            target = g * targets + j
-            value = mine[j * share : (j + 1) * share]
+    def amplitude(h, core):
+        parts = []
+        for g in range(groups):
+            both = jnp.dot(
+                turned[core, g * size : (g + 1) * size, :], split[h], preferred_element_type=F32
+            )
+            parts.append(both[:, :half] + both[:, half:])
+        return parts
+
+    def send_away(h):
+        for g, value in enumerate(amplitude(h, other)):
+            away[h, g * size : (g + 1) * size, :] = value
+        for g in range(groups):
+            part_copy(h, g).start()
+
+    def stay(h):
+        for g, value in enumerate(amplitude(h, b)):
+            mine[g * size : (g + 1) * size, :] = value
+
+    upper_half = (2 * a) // n_ka
+
+    def finish(h):
+        for g in range(groups):
+            part_copy(h, g).wait_recv()
+        for i in range(n_ka):
+            target = upper_half * i + (1 - upper_half) * (n_ka - 1 - i)
+            span = pl.ds(pl.multiple_of(target * share, share), share)
+            value = mine[span, :] + part[h, span, :]
 
             @pl.when(target == a)
             def _():
@@ -311,7 +335,7 @@
             def _():
                 peak = jnp.maximum(jnp.max(jnp.abs(value), axis=0, keepdims=True), TINY)
                 zsend[h, target] = jnp.round(value * (LEVELS / peak)).astype(jnp.int16)
-                ssend[h, target] = jnp.broadcast_to(peak / LEVELS, (8, half))
+                ssend[h, target] = peak / LEVELS
                 for copy in out_copies(h, a, target):
                     copy.start()
 
@@ -328,19 +352,17 @@
         total = out_ref[:, half_lanes(h)]
         for d in range(1, n_ka):
             sender = lax.rem(a + d, n_ka)
-            total = total + zrecv[h, sender].astype(F32) * srecv[h, sender, 0:1, :]
+            total = total + zrecv[h, sender].astype(F32) * srecv[h, sender]
         out_ref[:, half_lanes(h)] = total
 
     own_half(0, 0)
     if n_half > 1:
         own_half(0, 1)
     own_half(1, 0)
-    for h in range(1, n_half):
-        start_edges(h)
     if n_half > 1:
         own_half(1, 1)
-    for j in range(chunks):
-        if j > 0 or chunks == 1:
+    for j in chunks(0):
+        if j == len(cuts[0]) - 2:
             turn_initial()
         relay(0, j)
         if j == 0 and rounds > 0:
@@ -353,7 +375,7 @@
     for h in range(n_half):
         if h == 0:
             take(h, b, 0, rows)
-            for j in range(chunks):
+            for j in chunks(h):
                 forward(h, j).wait_recv()
             take(h, other, 0, rows, last_take=True)
             for r in range(1, rounds + 1):
@@ -363,18 +385,16 @@
                 for side in range(2):
                     await_token(side, r)
         else:
-            for j in range(chunks):
+            for j in chunks(h):
                 relay(h, j)
-                take(h, b, j * step, step)
-                if j > 0:
-                    forward(h, j - 1).wait_recv()
-                    take(h, other, (j - 1) * step, step)
-            forward(h, chunks - 1).wait_recv()
-            take(h, other, rows - step, step, last_take=True)
-        for g in range(groups):
-            send_away(h, g)
-        for g in range(groups):
-            finish(h, g)
+                take(h, b, *chunk(h, j))
+                if j > 1:
+                    take_other(h, j - 2)
+            for j in list(chunks(h))[-2:]:
+                take_other(h, j)
+        send_away(h)
+        stay(h)
+        finish(h)
     for h in range(n_half):
         add_sums(h)
 
@@ -408,12 +428,13 @@
     share = states // (2 * n_ka)
     n_half = max(1, width // 128)
     half = width // n_half
-    chunks = 2
+    cuts = [[0, rows // 2, rows]] * n_half
+    most = max(len(c) for c in cuts) - 1
     groups = 2
     dma = pltpu.SemaphoreType.DMA
     vmem = pltpu.VMEM
     amplitude = pl.pallas_call(
-        functools.partial(kernel, n_ka, n_half, chunks, groups),
+        functools.partial(kernel, n_ka, n_half, cuts, groups),
         out_shape=vmem((share, width), F32),
         in_specs=[pl.BlockSpec(memory_space=pl.ANY)] * 4,
         out_specs=pl.BlockSpec(memory_space=pltpu.VMEM),
@@ -427,11 +448,12 @@
             vmem((n_half, rows, kblocks * half), F32),
             vmem((n_half, kblocks * rows, 2 * half), BF16),
             vmem((n_half, n_ka * share, half), F32),
+            vmem((n_ka * share, half), F32),
             vmem((n_half, n_ka * share, half), F32),
             vmem((n_half, n_ka, share, half), jnp.int16),
             vmem((n_half, n_ka, share, half), jnp.int16),
-            vmem((n_half, n_ka, 8, half), F32),
-            vmem((n_half, n_ka, 8, half), F32),
+            vmem((n_half, n_ka, 1, half), F32),
+            vmem((n_half, n_ka, 1, half), F32),
             vmem((2, 8, half), jnp.int32),
             vmem((2, 8, half), jnp.int32),
             dma(()),
@@ -441,11 +463,11 @@
             dma((n_half,)),
             dma((n_half,)),
             dma((2,)),
-            dma((2, n_half, chunks)),
+            dma((2, n_half, most)),
             dma((2,)),
             dma((2,)),
             dma(()),
-            dma((n_half, chunks)),
+            dma((n_half, most)),
             dma(()),
             dma((n_half, groups)),
             dma(()),

time: 27.5 us -> 26.6 us (0.967)
  Pallas kernels: 26.7 us -> 25.7 us
    pallas_call x1, Pallas kernels: 26.7 us -> 25.7 us  [on_device(): pl.pallas_call(functools.partial(kernel, n_ka, n_half, cuts, groups), out...]
where the time goes in v5:
time: 26.6 us; the launch traced here: 26.4 us
  Pallas kernels  25.7 us (97%)
  other arithmetic  0.67 us (3%)
    pallas_call x1, Pallas kernels, on_device(): pl.pallas_call(functools.partial(kernel, n_ka, n_half, cuts, groups), out...  25.7 us
    mul x1, other arithmetic, on_device(): return amplitude * amplitude  0.67 us

profile of v5, /device:TPU:0, one launch (start us, length us, event | category | flops | bytes accessed | tf_op | source)
XLA Modules:
  0.0 26.4 jit_solution(8169108253549459771)
XLA Ops:
  0.0 25.7 %shard_map.46 = f32[128,256]{1,0:T(8,128)S(1)} custom-call(s32[2]{0:T(128)} %counts_hbm.1, bf16[2,1024,2048]{2,1,0:T(8,128)(2,1)} %moments_hbm.1, bf16[2,1024,1024]{2,1,0:T(8,128)(2,1)} %initial_hbm.1, bf16[2,1024,256]{2,1,0:T(8,128)(2,1)} %final_hbm.1), custom_call_target="tpu_custom_call" | custom-call | tf_op jit(solution)/shard_map/pallas_call | solution.py:436
  25.8 0.7 %mul.3 = f32[128,256]{1,0:T(8,128)} multiply(f32[128,256]{1,0:T(8,128)S(1)} %shard_map.46, f32[128,256]{1,0:T(8,128)S(1)} %shard_map.46) | non-fusion elementwise | flops 32768 | bytes 393216 | tf_op jit(solution)/shard_map/mul | solution.py:484

commit v6 on v5

--- a/solution.py
+++ b/solution.py
@@ -158,10 +158,14 @@
             @pl.when(sends[side])
             def _():
                 count_copy(side).start()
-        for h in range(n_half):
-            start_edges(h)
+        start_edges(0)
         for h in range(n_half):
             own_copy(h).start()
+
+        @pl.when(b == 0)
+        def _():
+            for h in range(1, n_half):
+                start_edges(h)
 
     start_loads()
     greet()
@@ -364,6 +368,11 @@
     for j in chunks(0):
         if j == len(cuts[0]) - 2:
             turn_initial()
+
+            @pl.when(b == 1)
+            def _():
+                for h in range(1, n_half):
+                    start_edges(h)
         relay(0, j)
         if j == 0 and rounds > 0:
             for side in range(2):

time: 26.6 us -> 26.3 us (0.989)
    pallas_call x1, Pallas kernels: 25.7 us -> 25.5 us  [on_device(): pl.pallas_call(functools.partial(kernel, n_ka, n_half, cuts, groups), out...]
where the time goes in v6:
time: 26.3 us; the launch traced here: 26.1 us
  Pallas kernels  25.5 us (97%)
  other arithmetic  0.67 us (3%)
    pallas_call x1, Pallas kernels, on_device(): pl.pallas_call(functools.partial(kernel, n_ka, n_half, cuts, groups), out...  25.5 us
    mul x1, other arithmetic, on_device(): return amplitude * amplitude  0.67 us

profile of v6, /device:TPU:0, one launch (start us, length us, event | category | flops | bytes accessed | tf_op | source)
XLA Modules:
  0.0 26.1 jit_solution(148224545223465253)
XLA Ops:
  0.0 25.5 %shard_map.46 = f32[128,256]{1,0:T(8,128)S(1)} custom-call(s32[2]{0:T(128)} %counts_hbm.1, bf16[2,1024,2048]{2,1,0:T(8,128)(2,1)} %moments_hbm.1, bf16[2,1024,1024]{2,1,0:T(8,128)(2,1)} %initial_hbm.1, bf16[2,1024,256]{2,1,0:T(8,128)(2,1)} %final_hbm.1), custom_call_target="tpu_custom_call" | custom-call | tf_op jit(solution)/shard_map/pallas_call | solution.py:445
  25.5 0.7 %mul.3 = f32[128,256]{1,0:T(8,128)} multiply(f32[128,256]{1,0:T(8,128)S(1)} %shard_map.46, f32[128,256]{1,0:T(8,128)S(1)} %shard_map.46) | non-fusion elementwise | flops 32768 | bytes 393216 | tf_op jit(solution)/shard_map/mul | solution.py:493

commit v7 on v6

--- a/solution.py
+++ b/solution.py
@@ -28,9 +28,9 @@
 
 def kernel(
     n_ka, n_half, cuts, groups, counts_hbm, moments_hbm, initial_hbm, final_hbm, out_ref,
-    counts, mom, ini, turned, own, edge, comb, split, away, mine, part, zsend, zrecv, ssend, srecv, csend, crecv,
+    counts, mom, ini, turned, own, edge, comb, split, away, away_scale, mine, part, part_scale, zsend, zrecv, ssend, srecv, csend, crecv,
     counts_sem, mom_sem, ini_sem, own_sem, own_send, own_recv, z_send, z_recv, count_send, count_recv,
-    fwd_send, fwd_recv, part_send, part_recv, out_send, out_recv, scale_send, scale_recv,
+    fwd_send, fwd_recv, part_send, part_recv, part_scale_send, part_scale_recv, out_send, out_recv, scale_send, scale_recv,
     token_up, token_down,
 ):
     kblocks, rows, states = ini.shape
@@ -273,15 +273,28 @@
     targets = n_ka // groups
     size = targets * share
 
-    def part_copy(h, g):
-        return pltpu.make_async_remote_copy(
-            src_ref=away.at[h, pl.ds(g * size, size)],
-            dst_ref=part.at[h, pl.ds(g * size, size)],
+    def part_copies(h):
+        values = pltpu.make_async_remote_copy(
+            src_ref=away.at[h],
+            dst_ref=part.at[h],
             send_sem=part_send,
-            recv_sem=part_recv.at[h, g],
+            recv_sem=part_recv.at[h],
             device_id={"vib": other},
             device_id_type=MESH,
         )
+        scales = pltpu.make_async_remote_copy(
+            src_ref=away_scale.at[h],
+            dst_ref=part_scale.at[h],
+            send_sem=part_scale_send,
+            recv_sem=part_scale_recv.at[h],
+            device_id={"vib": other},
+            device_id_type=MESH,
+        )
+        return values, scales
+
+    def pack(value):
+        peak = jnp.maximum(jnp.max(jnp.abs(value), axis=0, keepdims=True), TINY)
+        return jnp.round(value * (LEVELS / peak)).astype(jnp.int16), peak / LEVELS
 
     def out_copies(h, sender, target):
         values = pltpu.make_async_remote_copy(
@@ -313,23 +326,26 @@
 
     def send_away(h):
         for g, value in enumerate(amplitude(h, other)):
-            away[h, g * size : (g + 1) * size, :] = value
-        for g in range(groups):
-            part_copy(h, g).start()
+            away[h, g * size : (g + 1) * size, :], away_scale[h, g] = pack(value)
+        for copy in part_copies(h):
+            copy.start()
 
     def stay(h):
         for g, value in enumerate(amplitude(h, b)):
             mine[g * size : (g + 1) * size, :] = value
+        for copy in part_copies(h):
+            copy.wait_recv()
+        for g in range(groups):
+            span = pl.ds(g * size, size)
+            mine[span, :] = mine[span, :] + part[h, span, :].astype(F32) * part_scale[h, g]
 
     upper_half = (2 * a) // n_ka
 
     def finish(h):
-        for g in range(groups):
-            part_copy(h, g).wait_recv()
         for i in range(n_ka):
             target = upper_half * i + (1 - upper_half) * (n_ka - 1 - i)
             span = pl.ds(pl.multiple_of(target * share, share), share)
-            value = mine[span, :] + part[h, span, :]
+            value = mine[span, :]
 
             @pl.when(target == a)
             def _():
@@ -337,9 +353,7 @@
 
             @pl.when(target != a)
             def _():
-                peak = jnp.maximum(jnp.max(jnp.abs(value), axis=0, keepdims=True), TINY)
-                zsend[h, target] = jnp.round(value * (LEVELS / peak)).astype(jnp.int16)
-                ssend[h, target] = peak / LEVELS
+                zsend[h, target], ssend[h, target] = pack(value)
                 for copy in out_copies(h, a, target):
                     copy.start()
 
@@ -421,7 +435,7 @@
             own_copy(h).wait_send()
             all_out(zsend, h, out_send, out_recv.at[h]).wait_send()
             all_out(ssend, h, scale_send, scale_recv.at[h]).wait_send()
-        for buffer, sem in ((edge.at[:, rows_of(b)], fwd_send), (away, part_send)):
+        for buffer, sem in ((edge.at[:, rows_of(b)], fwd_send), (away, part_send), (away_scale, part_scale_send)):
             pltpu.make_async_remote_copy(
                 src_ref=buffer, dst_ref=buffer, send_sem=sem, recv_sem=sem,
                 device_id={"vib": other}, device_id_type=MESH,
@@ -456,9 +470,11 @@
             vmem((n_half, whole, 2 * half), BF16),
             vmem((n_half, rows, kblocks * half), F32),
             vmem((n_half, kblocks * rows, 2 * half), BF16),
-            vmem((n_half, n_ka * share, half), F32),
+            vmem((n_half, n_ka * share, half), jnp.int16),
+            vmem((n_half, groups, 1, half), F32),
             vmem((n_ka * share, half), F32),
-            vmem((n_half, n_ka * share, half), F32),
+            vmem((n_half, n_ka * share, half), jnp.int16),
+            vmem((n_half, groups, 1, half), F32),
             vmem((n_half, n_ka, share, half), jnp.int16),
             vmem((n_half, n_ka, share, half), jnp.int16),
             vmem((n_half, n_ka, 1, half), F32),
@@ -478,7 +494,9 @@
             dma(()),
             dma((n_half, most)),
             dma(()),
-            dma((n_half, groups)),
+            dma((n_half,)),
+            dma(()),
+            dma((n_half,)),
             dma(()),
             dma((n_half,)),
             dma(()),

time: 26.3 us -> 26.2 us (level)
  no operation moved by 1% of the time
where the time goes in v7:
time: 26.2 us; the launch traced here: 26.1 us
  Pallas kernels  25.4 us (97%)
  other arithmetic  0.67 us (3%)
    pallas_call x1, Pallas kernels, on_device(): pl.pallas_call(functools.partial(kernel, n_ka, n_half, cuts, groups), out...  25.4 us
    mul x1, other arithmetic, on_device(): return amplitude * amplitude  0.67 us

profile of v7, /device:TPU:0, one launch (start us, length us, event | category | flops | bytes accessed | tf_op | source)
XLA Modules:
  0.0 26.1 jit_solution(10708311630231641188)
XLA Ops:
  0.0 25.4 %shard_map.46 = f32[128,256]{1,0:T(8,128)S(1)} custom-call(s32[2]{0:T(128)} %counts_hbm.1, bf16[2,1024,2048]{2,1,0:T(8,128)(2,1)} %moments_hbm.1, bf16[2,1024,1024]{2,1,0:T(8,128)(2,1)} %initial_hbm.1, bf16[2,1024,256]{2,1,0:T(8,128)(2,1)} %final_hbm.1), custom_call_target="tpu_custom_call" | custom-call | tf_op jit(solution)/shard_map/pallas_call | solution.py:459
  25.4 0.7 %mul.3 = f32[128,256]{1,0:T(8,128)} multiply(f32[128,256]{1,0:T(8,128)S(1)} %shard_map.46, f32[128,256]{1,0:T(8,128)S(1)} %shard_map.46) | non-fusion elementwise | flops 32768 | bytes 393216 | tf_op jit(solution)/shard_map/mul | solution.py:511

commit v8 on v6

--- a/solution.py
+++ b/solution.py
@@ -273,12 +273,12 @@
     targets = n_ka // groups
     size = targets * share
 
-    def part_copy(h, g):
+    def part_copy(h):
         return pltpu.make_async_remote_copy(
-            src_ref=away.at[h, pl.ds(g * size, size)],
-            dst_ref=part.at[h, pl.ds(g * size, size)],
+            src_ref=away.at[h],
+            dst_ref=part.at[h],
             send_sem=part_send,
-            recv_sem=part_recv.at[h, g],
+            recv_sem=part_recv.at[h],
             device_id={"vib": other},
             device_id_type=MESH,
         )
@@ -314,8 +314,7 @@
     def send_away(h):
         for g, value in enumerate(amplitude(h, other)):
             away[h, g * size : (g + 1) * size, :] = value
-        for g in range(groups):
-            part_copy(h, g).start()
+        part_copy(h).start()
 
     def stay(h):
         for g, value in enumerate(amplitude(h, b)):
@@ -324,8 +323,7 @@
     upper_half = (2 * a) // n_ka
 
     def finish(h):
-        for g in range(groups):
-            part_copy(h, g).wait_recv()
+        part_copy(h).wait_recv()
         for i in range(n_ka):
             target = upper_half * i + (1 - upper_half) * (n_ka - 1 - i)
             span = pl.ds(pl.multiple_of(target * share, share), share)
@@ -478,7 +476,7 @@
             dma(()),
             dma((n_half, most)),
             dma(()),
-            dma((n_half, groups)),
+            dma((n_half,)),
             dma(()),
             dma((n_half,)),
             dma(()),

time: 26.3 us -> 26.3 us (level)
  no operation moved by 1% of the time
where the time goes in v8:
time: 26.3 us; the launch traced here: 26.1 us
  Pallas kernels  25.4 us (97%)
  other arithmetic  0.67 us (3%)
    pallas_call x1, Pallas kernels, on_device(): pl.pallas_call(functools.partial(kernel, n_ka, n_half, cuts, groups), out...  25.4 us
    mul x1, other arithmetic, on_device(): return amplitude * amplitude  0.67 us

profile of v8, /device:TPU:0, one launch (start us, length us, event | category | flops | bytes accessed | tf_op | source)
XLA Modules:
  0.0 26.1 jit_solution(13465200116909914563)
XLA Ops:
  0.0 25.4 %shard_map.46 = f32[128,256]{1,0:T(8,128)S(1)} custom-call(s32[2]{0:T(128)} %counts_hbm.1, bf16[2,1024,2048]{2,1,0:T(8,128)(2,1)} %moments_hbm.1, bf16[2,1024,1024]{2,1,0:T(8,128)(2,1)} %initial_hbm.1, bf16[2,1024,256]{2,1,0:T(8,128)(2,1)} %final_hbm.1), custom_call_target="tpu_custom_call" | custom-call | tf_op jit(solution)/shard_map/pallas_call | solution.py:443
  25.4 0.7 %mul.3 = f32[128,256]{1,0:T(8,128)} multiply(f32[128,256]{1,0:T(8,128)S(1)} %shard_map.46, f32[128,256]{1,0:T(8,128)S(1)} %shard_map.46) | non-fusion elementwise | flops 32768 | bytes 393216 | tf_op jit(solution)/shard_map/mul | solution.py:491
